TPU v7x, 128 devices: a whole 4x4x4 slice. The times are simulated.
128 devices in a mesh: seq: 16 (over z, x), hid: 4 (over y), rep: 2 (over core).
Axes of the slice: x: 4, y: 4, z: 4, core: 2. Of those that a mesh axis runs over, the one named last changes fastest.
Arguments:
- tokens: bfloat16 [16384, 5376], P(('rep', 'seq'), 'hid'), parts along dimension 0, may hold values from -6 to 6
- norm_gain: float32 [5376], replicated, may hold values from 0.1 to 1.9
- w_query: bfloat16 [5376, 4096], P('seq', 'hid'), may hold values from -0.078125 to 0.078125
- w_key: bfloat16 [5376, 2048], P('seq', 'hid'), may hold values from -0.078125 to 0.078125
- w_value: bfloat16 [5376, 2048], P('seq', 'hid'), may hold values from -0.078125 to 0.078125
- query_gain: float32 [128], replicated, may hold values from 0.5 to 8
- key_gain: float32 [128], replicated, may hold values from 0.5 to 8
- w_out: bfloat16 [4096, 5376], P('hid', 'seq'), may hold values from -0.09375 to 0.09375
Outputs:
- attended: bfloat16 [16384, 5376], P(('rep', 'seq'), 'hid'), parts along dimension 0
There are 2 independent parts, one for each index of `rep`. A program takes and returns all parts, laid end to end along the dimension named above; an argument that names none is the same for every part. Nothing has to cross between parts.
All inputs are finite; a program needn't handle non-finite values.
Results may differ from a plain program's by a relative error of at most 0.023.
The roundings to bfloat16 on the way count: a program that leaves them out, or rounds other values in their place, can miss the bound.
Values may be sent and summed in bfloat16 or wider, within the bound.
A program may use at most 128 MiB of HBM per device.

v0:
```python
import jax
import jax.numpy as jnp
from jax import lax
from jax.sharding import PartitionSpec as P

HEAD_WIDTH = 128
WINDOW = 1024
QSCALE = 168
DEPTH = 2


def shifted(x, axis, by):
    count = lax.axis_size(axis)
    pairs = [(i, i + by) for i in range(count) if 0 <= i + by < count]
    return lax.ppermute(x, axis, pairs)


def rope(heads, positions):
    half = heads.shape[-1] // 2
    freq = 10000.0 ** (-(jnp.arange(half, dtype=jnp.float32) * 2.0) / heads.shape[-1])
    angle = positions[:, None] * freq[None, :]
    cosine = jnp.cos(angle)[:, None, :]
    sine = jnp.sin(angle)[:, None, :]
    first = heads[..., :half]
    second = heads[..., half:]
    return jnp.concatenate(
        [first * cosine - second * sine, second * cosine + first * sine], axis=-1
    )


def head_norm(heads, gain):
    return heads * lax.rsqrt(jnp.mean(heads * heads, axis=-1, keepdims=True) + 1e-06) * gain


def add_rows(normed, piece):
    return jnp.dot(normed, piece, preferred_element_type=jnp.float32)


def shards(tokens, norm_gain, w_query, w_key, w_value, query_gain, key_gain, w_out):
    whole = lax.all_gather(tokens, "hid", axis=1, tiled=True)
    xfloat = whole.astype(jnp.float32)
    normed = (
        xfloat * lax.rsqrt(jnp.mean(xfloat * xfloat, axis=-1, keepdims=True) + 1e-06) * norm_gain
    ).astype(jnp.bfloat16)
    rows = normed.shape[0]

    def add_one(piece):
        return add_rows(normed, piece)

    query = add_one(lax.all_gather(w_query, "seq", axis=0, tiled=True))
    key = add_one(lax.all_gather(w_key, "seq", axis=0, tiled=True))
    value = add_one(lax.all_gather(w_value, "seq", axis=0, tiled=True))
    local_heads = w_query.shape[1] // HEAD_WIDTH
    local_kv = w_key.shape[1] // HEAD_WIDTH
    base = lax.axis_index("seq") * rows
    qpos = base + jnp.arange(rows, dtype=jnp.int32)
    positions = qpos.astype(jnp.float32)
    qh = (
        rope(head_norm(query.reshape(rows, local_heads, HEAD_WIDTH), query_gain), positions)
        * QSCALE ** (-0.5)
    ).astype(jnp.bfloat16)
    kh = rope(head_norm(key.reshape(rows, local_kv, HEAD_WIDTH), key_gain), positions).astype(
        jnp.bfloat16
    )
    value_head = value.reshape(rows, local_kv, HEAD_WIDTH).astype(jnp.bfloat16)
    key_blocks = []
    value_blocks = []
    for distance in range(1, DEPTH + 1):
        arrived = shifted((kh, value_head), "seq", distance)
        key_blocks.insert(0, arrived[0])
        value_blocks.insert(0, arrived[1])
    keys = jnp.concatenate(key_blocks + [kh], axis=0)
    values = jnp.concatenate(value_blocks + [value_head], axis=0)
    window_extent = keys.shape[0]
    kpos = base - DEPTH * rows + jnp.arange(window_extent, dtype=jnp.int32)
    diff = qpos[:, None] - kpos[None, :]
    allowed = (diff >= 0) & (diff < WINDOW) & (kpos >= 0)[None, :]
    group = local_heads // local_kv
    grouped = qh.reshape(rows, local_kv, group, HEAD_WIDTH).transpose(1, 0, 2, 3)

    def one_head(operands):
        qpart, kpart, vpart = operands
        scores = jnp.einsum("rgd,ld->grl", qpart, kpart, preferred_element_type=jnp.float32)
        scores = jnp.where(allowed[None], scores, -jnp.inf)
        probs = jax.nn.softmax(scores, axis=-1).astype(jnp.bfloat16)
        mixed = jnp.einsum("grl,ld->rgd", probs, vpart, preferred_element_type=jnp.float32)
        return mixed.astype(jnp.bfloat16)

    per_head = lax.map(one_head, (grouped, keys.transpose(1, 0, 2), values.transpose(1, 0, 2)))
    heads_out = per_head.transpose(1, 0, 2, 3).reshape(rows, local_heads * HEAD_WIDTH)
    terms = jnp.dot(
        heads_out,
        lax.all_gather(w_out, "seq", axis=1, tiled=True),
        preferred_element_type=jnp.float32,
    )
    return lax.psum_scatter(terms.astype(jnp.bfloat16), "hid", scatter_dimension=1, tiled=True)


def solution(mesh):
    return jax.shard_map(
        shards,
        mesh=mesh,
        in_specs=(
            P(("rep", "seq"), "hid"),
            P(),
            P("seq", "hid"),
            P("seq", "hid"),
            P("seq", "hid"),
            P(),
            P(),
            P("hid", "seq"),
        ),
        out_specs=P(("rep", "seq"), "hid"),
        check_vma=False,
    )
```

profile of v0, /device:TPU:0, one launch (start us, length us, event | category | flops | bytes accessed | tf_op | source)
XLA Modules:
  0.0 466.1 jit_solution(10605443407271170900)
XLA Ops:
  11.0 59.7 %all-gather.6.cloned.1.call-done = bf16[512,5376]{0,1:T(8,128)(2,1)} async-done(((bf16[512,1344]{0,1:T(8,128)(2,1)}), bf16[512,5376]{0,1:T(8,128)(2,1)}) %all-gather.6.cloned.1.call-update) | async-done | bytes 5505040 | tf_op jit(solution)/shard_map/all_gather | solution.py:40
  70.7 3.8 fusion.41
  74.5 56.7 %all-gather.10.cloned.1.call-done = bf16[5376,512]{1,0:T(8,128)(2,1)} async-done(((bf16[336,512]{1,0:T(8,128)(2,1)}), bf16[5376,512]{1,0:T(8,128)(2,1)}) %all-gather.10.cloned.1.call-update) | async-done | bytes 5505040 | tf_op jit(solution)/shard_map/all_gather | solution.py:51
  131.2 7.6 %multiply_reduce_fusion.1 = (f32[512,4]{0,1:T(4,128)S(1)}, f32[512,512]{0,1:T(8,128)S(1)}) fusion(bf16[5376,512]{1,0:T(8,128)(2,1)} %all-gather.10.cloned.1.call-done, bf16[512,5376]{0,1:T(8,128)(2,1)} %all-gather.6.cloned.1.call-done, f32[5376]{0:T(1024)S(1)} %copy-done.2, f32[512]{0:T(512)S(1)} %add_rsqrt_fusion.2), kind=kOutput, calls=%fused_computation.52 | convolution fusion | flops 2830104576 | bytes 12090368 | tf_op jit(solution)/shard_map/dot_general | solution.py:36
  140.2 4.9 %collective-permute-start.2 = (bf16[512,4,128]{2,0,1:T(8,128)(2,1)S(1)}, bf16[512,4,128]{2,0,1:T(8,128)(2,1)S(1)}, u32[]{:S(2)}, u32[]{:S(2)}) collective-permute-start(bf16[512,4,128]{2,0,1:T(8,128)(2,1)S(1)} %pad_maximum_fusion), channel_id=1, source_target_pairs={{0,16},{8,24},{16,32},{24,40},{32,48},{40,56},{48,64},{56,72},{64,... | collective-permute-start | bytes 1572872 | tf_op jit(solution)/shard_map/ppermute | solution.py:15
  145.2 2.5 collective-permute-start.3
  147.7 54.3 %all-gather.8.cloned.1.call-done = bf16[5376,512]{1,0:T(8,128)(2,1)} async-done(((bf16[336,512]{1,0:T(8,128)(2,1)}), bf16[5376,512]{1,0:T(8,128)(2,1)}) %all-gather.8.cloned.1.call-update) | async-done | bytes 5505040 | tf_op jit(solution)/shard_map/all_gather | solution.py:52
  202.0 8.4 %convolution_convert_fusion.1 = bf16[512,512]{0,1:T(8,128)(2,1)} fusion(bf16[5376,512]{1,0:T(8,128)(2,1)} %all-gather.8.cloned.1.call-done, bf16[512,5376]{0,1:T(8,128)(2,1)} %all-gather.6.cloned.1.call-done, f32[5376]{0:T(1024)S(1)} %copy-done.2, f32[512]{0:T(512)S(1)} %add_rsqrt_fusion.2), kind=kOutput, calls=%fused_computation.47 | convolution fusion | flops 2829844480 | bytes 11557888 | tf_op jit(solution)/shard_map/dot_general | solution.py:36
  210.4 5.7 %collective-permute-start = (bf16[512,4,128]{0,2,1:T(8,128)(2,1)}, bf16[512,4,128]{0,2,1:T(8,128)(2,1)}, u32[]{:S(2)}, u32[]{:S(2)}) collective-permute-start(bf16[512,4,128]{0,2,1:T(8,128)(2,1)} %bitcast), channel_id=1, source_target_pairs={{0,16},{8,24},{16,32},{24,40},{32,48},{40,56},{48,64},{56,72},{64,... | collective-permute-start | bytes 1572872 | tf_op jit(solution)/shard_map/ppermute | solution.py:15
  216.1 3.3 collective-permute-start.1
  219.4 1.5 maximum_bitcast_fusion.1
  220.9 12.5 %collective-permute-done = bf16[512,4,128]{0,2,1:T(8,128)(2,1)} collective-permute-done((bf16[512,4,128]{0,2,1:T(8,128)(2,1)}, bf16[512,4,128]{0,2,1:T(8,128)(2,1)}, u32[]{:S(2)}, u32[]{:S(2)}) %collective-permute-start) | collective-permute-done | bytes 524320 | tf_op jit(solution)/shard_map/ppermute | solution.py:15
  233.4 14.5 %collective-permute-done.1 = bf16[512,4,128]{0,2,1:T(8,128)(2,1)} collective-permute-done((bf16[512,4,128]{0,2,1:T(8,128)(2,1)}, bf16[512,4,128]{0,2,1:T(8,128)(2,1)}, u32[]{:S(2)}, u32[]{:S(2)}) %collective-permute-start.1) | collective-permute-done | bytes 524320 | tf_op jit(solution)/shard_map/ppermute | solution.py:15
  247.9 2.6 maximum_bitcast_fusion
  250.5 55.1 %all-gather.12.cloned.1.call-done = bf16[5376,1024]{1,0:T(8,128)(2,1)} async-done(((bf16[336,1024]{1,0:T(8,128)(2,1)}), bf16[5376,1024]{1,0:T(8,128)(2,1)}) %all-gather.12.cloned.1.call-update) | async-done | bytes 11010064 | tf_op jit(solution)/shard_map/all_gather | solution.py:50
  305.6 11.7 %convolution_bitcast_fusion = f32[64,8,8,128]{3,1,2,0:T(8,128)S(1)} fusion(bf16[5376,1024]{1,0:T(8,128)(2,1)} %all-gather.12.cloned.1.call-done, bf16[512,5376]{0,1:T(8,128)(2,1)} %all-gather.6.cloned.1.call-done, f32[5376]{0:T(1024)S(1)} %copy-done.2, f32[512]{0:T(512)S(1)} %add_rsqrt_fusion.2), kind=kOutput, calls=%fused_computation.44 | convolution fusion | flops 5648154624 | bytes 18635776 | tf_op jit(solution)/shard_map/dot_general | solution.py:36
  322.8 43.4 %while.11 = (s32[]{:T(128)}, bf16[4,512,2,128]{1,3,2,0:T(8,128)(2,1)S(1)}, bf16[4,1536,128]{1,2,0:T(8,128)(2,1)}, bf16[4,1536,128]{2,1,0:T(8,128)(2,1)}, bf16[4,...) while((s32[]{:T(128)}, ...), condition=%wide.region_6.7_spmd.clone, body=%wide.region_3.6_spmd.clone.sunk | while | flops 817235456 | bytes 15486557 | solution.py:89
  322.8 1.2 fusion.74
  324.0 5.8 %fusion.75 = (f32[2,512]{1,0:T(2,128)S(1)}, f32[2,512,1536]{1,2,0:T(8,128)}) fusion(pred[512,1536]{0,1:T(8,128)(4,1)S(1)} %fusion.74, bf16[4,1536,128]{2,1,0:T(8,128)(2,1)} %get-tuple-element.159, s32[]{:T(128)} %get-tuple-element.147, bf16[4,512,2,128]{3,1,2,0:T(8,128)(2,1)S(1)} %get-tuple-element.160), kind=kOutput, calls=%fused_computation.65.clone.1 | convolution fusion | flops 407373312 | bytes 7738368 | tf_op jit(solution)/shard_map/while/body/eval_jaxpr/sub | solution.py:85
  329.8 3.6 fusion.76
  333.5 1.2 fusion.74
  334.7 5.8 %fusion.75 = (f32[2,512]{1,0:T(2,128)S(1)}, f32[2,512,1536]{1,2,0:T(8,128)}) fusion(pred[512,1536]{0,1:T(8,128)(4,1)S(1)} %fusion.74, bf16[4,1536,128]{2,1,0:T(8,128)(2,1)} %get-tuple-element.159, s32[]{:T(128)} %get-tuple-element.147, bf16[4,512,2,128]{3,1,2,0:T(8,128)(2,1)S(1)} %get-tuple-element.160), kind=kOutput, calls=%fused_computation.65.clone.1 | convolution fusion | flops 407373312 | bytes 7738368 | tf_op jit(solution)/shard_map/while/body/eval_jaxpr/sub | solution.py:85
  340.5 4.4 fusion.76
  345.0 1.2 fusion.74
  346.2 5.8 %fusion.75 = (f32[2,512]{1,0:T(2,128)S(1)}, f32[2,512,1536]{1,2,0:T(8,128)}) fusion(pred[512,1536]{0,1:T(8,128)(4,1)S(1)} %fusion.74, bf16[4,1536,128]{2,1,0:T(8,128)(2,1)} %get-tuple-element.159, s32[]{:T(128)} %get-tuple-element.147, bf16[4,512,2,128]{3,1,2,0:T(8,128)(2,1)S(1)} %get-tuple-element.160), kind=kOutput, calls=%fused_computation.65.clone.1 | convolution fusion | flops 407373312 | bytes 7738368 | tf_op jit(solution)/shard_map/while/body/eval_jaxpr/sub | solution.py:85
  352.0 3.6 fusion.76
  355.6 1.2 fusion.74
  356.8 5.8 %fusion.75 = (f32[2,512]{1,0:T(2,128)S(1)}, f32[2,512,1536]{1,2,0:T(8,128)}) fusion(pred[512,1536]{0,1:T(8,128)(4,1)S(1)} %fusion.74, bf16[4,1536,128]{2,1,0:T(8,128)(2,1)} %get-tuple-element.159, s32[]{:T(128)} %get-tuple-element.147, bf16[4,512,2,128]{3,1,2,0:T(8,128)(2,1)S(1)} %get-tuple-element.160), kind=kOutput, calls=%fused_computation.65.clone.1 | convolution fusion | flops 407373312 | bytes 7738368 | tf_op jit(solution)/shard_map/while/body/eval_jaxpr/sub | solution.py:85
  362.6 3.5 fusion.76
  366.2 23.9 %all-gather.14.cloned.1.call-done = bf16[1024,5376]{0,1:T(8,128)(2,1)} async-done(((bf16[1024,336]{0,1:T(8,128)(2,1)}), bf16[1024,5376]{0,1:T(8,128)(2,1)}) %all-gather.14.cloned.1.call-update) | async-done | bytes 11010064 | tf_op jit(solution)/shard_map/all_gather | solution.py:93
  390.1 11.8 %convolution_convert_fusion = bf16[512,5376]{0,1:T(8,128)(2,1)} fusion(bf16[1024,5376]{0,1:T(8,128)(2,1)} %all-gather.14.cloned.1.call-done, bf16[512,1024]{0,1:T(8,128)(2,1)S(1)} %bitcast.83), kind=kOutput, calls=%fused_computation.37 | convolution fusion | flops 5639897088 | bytes 17563648 | tf_op jit(solution)/shard_map/dot_general | solution.py:91
  402.0 57.3 %reduce-scatter.2.cloned.1.call-done = bf16[512,1344]{0,1:T(8,128)(2,1)} async-done(((bf16[512,5376]{0,1:T(8,128)(2,1)}), bf16[512,1344]{0,1:T(8,128)(2,1)}) %reduce-scatter.2.cloned.1.call-update) | async-done | bytes 1376272 | tf_op jit(solution)/shard_map/reduce_scatter | solution.py:96
  (45 shorter events, 11.2 us)
Async XLA Ops:
  6.5 64.2 %all-gather.6.cloned.1.call-start = ((), (), s32[]{:S(2)}) async-start(), calls=%async_computation.1 | async-start | bytes 6881280 | tf_op jit(solution)/shard_map/all_gather | solution.py:40
  7.3 123.9 %all-gather.10.cloned.1.call-start = ((), (), s32[]{:S(2)}) async-start(), calls=%async_computation.3 | async-start | bytes 5849088 | tf_op jit(solution)/shard_map/all_gather | solution.py:51
  8.0 194.0 %all-gather.8.cloned.1.call-start = ((), (), s32[]{:S(2)}) async-start(), calls=%async_computation.2 | async-start | bytes 5849088 | tf_op jit(solution)/shard_map/all_gather | solution.py:52
  8.7 296.9 %all-gather.12.cloned.1.call-start = ((), (), s32[]{:S(2)}) async-start(), calls=%async_computation.4 | async-start | bytes 11698176 | tf_op jit(solution)/shard_map/all_gather | solution.py:50
  9.3 380.8 %all-gather.14.cloned.1.call-start = ((), (), s32[]{:S(2)}) async-start(), calls=%async_computation.5 | async-start | bytes 11698176 | tf_op jit(solution)/shard_map/all_gather | solution.py:93
  9.9 121.3 %copy-start.2 = (f32[5376]{0:T(1024)S(1)}, f32[5376]{0:T(1024)}, u32[]{:S(2)}) copy-start(f32[5376]{0:T(1024)} %param.11) | copy-start | bytes 64516
  9.9 449.3 %reduce-scatter.2.cloned.1.call-start = ((), (), s32[]{:S(2)}) async-start(), calls=%async_computation.6 | async-start | bytes 6881280 | tf_op jit(solution)/shard_map/reduce_scatter | solution.py:96
  74.5 64.7 %copy-start = (f32[128]{0:T(128)S(1)}, f32[128]{0:T(128)}, u32[]{:S(2)}) copy-start(f32[128]{0:T(128)} %param.16) | copy-start | bytes 1540
  140.2 79.1 %collective-permute-start.2 = (bf16[512,4,128]{2,0,1:T(8,128)(2,1)S(1)}, bf16[512,4,128]{2,0,1:T(8,128)(2,1)S(1)}, u32[]{:S(2)}, u32[]{:S(2)}) collective-permute-start(bf16[512,4,128]{2,0,1:T(8,128)(2,1)S(1)} %pad_maximum_fusion), channel_id=1, source_target_pairs={{0,16},{8,24},{16,32},{24,40},{32,48},{40,56},{48,64},{56,72},{64,... | collective-permute-start | bytes 1572872 | tf_op jit(solution)/shard_map/ppermute | solution.py:15
  145.2 74.2 %collective-permute-start.3 = (bf16[512,4,128]{2,0,1:T(8,128)(2,1)S(1)}, bf16[512,4,128]{2,0,1:T(8,128)(2,1)S(1)}, u32[]{:S(2)}, u32[]{:S(2)}) collective-permute-start(bf16[512,4,128]{2,0,1:T(8,128)(2,1)S(1)} %pad_maximum_fusion), channel_id=1, source_target_pairs={{0,8},{8,16},{16,24},{24,32},{32,40},{40,48},{48,56},{56,64},{64,7... | collective-permute-start | bytes 1572872 | tf_op jit(solution)/shard_map/ppermute | solution.py:15
  210.4 23.1 %collective-permute-start = (bf16[512,4,128]{0,2,1:T(8,128)(2,1)}, bf16[512,4,128]{0,2,1:T(8,128)(2,1)}, u32[]{:S(2)}, u32[]{:S(2)}) collective-permute-start(bf16[512,4,128]{0,2,1:T(8,128)(2,1)} %bitcast), channel_id=1, source_target_pairs={{0,16},{8,24},{16,32},{24,40},{32,48},{40,56},{48,64},{56,72},{64,... | collective-permute-start | bytes 1572872 | tf_op jit(solution)/shard_map/ppermute | solution.py:15
  216.1 31.8 %collective-permute-start.1 = (bf16[512,4,128]{0,2,1:T(8,128)(2,1)}, bf16[512,4,128]{0,2,1:T(8,128)(2,1)}, u32[]{:S(2)}, u32[]{:S(2)}) collective-permute-start(bf16[512,4,128]{0,2,1:T(8,128)(2,1)} %bitcast), channel_id=1, source_target_pairs={{0,8},{8,16},{16,24},{24,32},{32,40},{40,48},{48,56},{56,64},{64,7... | collective-permute-start | bytes 1572872 | tf_op jit(solution)/shard_map/ppermute | solution.py:15
  317.3 1.4 copy-start.1
  321.6 1.2 copy-start.3
Sparse Core Ops, SparseCore 0:
  9.0 61.6 all-gather.5
  72.8 58.3 all-gather.9
  133.3 68.5 all-gather.7
  204.0 101.6 all-gather.11
  307.6 82.4 all-gather.13
  402.1 57.1 reduce-scatter.1
where the time goes:
time: 467 us; the launch traced here: 466 us
  waiting for transfers between devices  337 us (72%)
  matrix products  77.9 us (17%)
  other arithmetic  18.1 us (4%)
  starting transfers between devices  16.6 us (4%)
  between operations  13.7 us (3%)
    all_gather x1, waiting for transfers between devices, shards(): whole = lax.all_gather(tokens, 'hid', axis=1, tiled=True)  59.7 us
    reduce_scatter x1, waiting for transfers between devices, shards(): lax.psum_scatter(terms.astype(jnp.bfloat16), 'hid', scatter_dimension=1,...  57.3 us
    all_gather x1, waiting for transfers between devices, shards(): key = add_one(lax.all_gather(w_key, 'seq', axis=0, tiled=True))  56.7 us
    all_gather x1, waiting for transfers between devices, shards(): query = add_one(lax.all_gather(w_query, 'seq', axis=0, tiled=True))  55.1 us
    all_gather x1, waiting for transfers between devices, shards(): value = add_one(lax.all_gather(w_value, 'seq', axis=0, tiled=True))  54.3 us
    dot_general x3, matrix products, add_rows(): return jnp.dot(normed, piece, preferred_element_type=jnp.float32)  27.7 us
    ppermute x4, waiting for transfers between devices, shifted(): return lax.ppermute(x, axis, pairs)  27 us
    all_gather x1, waiting for transfers between devices, shards(): lax.all_gather(w_out, 'seq', axis=1, tiled=True)  23.9 us
  transfers between devices with their start and end apart: 10, of which 8 were waited for; matrix products, arithmetic and copies ran while one was open for 18% of the time, Pallas kernels for 0%

commit v1 on v0

v1 whole, which is shorter than its diff:
```python
import functools

import jax
import jax.numpy as jnp
from jax import lax
from jax.experimental import pallas as pl
from jax.experimental.pallas import tpu as pltpu
from jax.sharding import PartitionSpec as P

HEAD_WIDTH = 128
WINDOW = 1024
QSCALE = 168
DEPTH = 2
RING = 4
MESH = pl.DeviceIdType.MESH
BF16 = jnp.bfloat16
F32 = jnp.float32


def place():
    seq = lax.axis_index("seq")
    return lax.rem(seq, RING), lax.axis_index("hid"), lax.div(seq, RING), lax.axis_index("rep")


def device(x, y, z, r):
    return {"seq": z * RING + x, "hid": y, "rep": r}


def step(a, by):
    return lax.rem(a + by + RING, RING)


def send(src, dst, send_sem, recv_sem, dev):
    copy = pltpu.make_async_remote_copy(
        src_ref=src,
        dst_ref=dst,
        send_sem=send_sem,
        recv_sem=recv_sem,
        device_id=dev,
        device_id_type=MESH,
    )
    copy.start()
    return copy


def greet(devs):
    barrier = pltpu.get_barrier_semaphore()
    for dev in devs:
        pl.semaphore_signal(barrier, inc=1, device_id=dev, device_id_type=MESH)
    pl.semaphore_wait(barrier, len(devs))


def project_kernel(
    tok_ref, gain_ref, wcat_ref, qg_ref, kg_ref, cos_ref, sin_ref,
    q_ref, k_ref, v_ref,
    wbuf, xbuf, acc, sums,
    wsend, wrecv, sib_send, sib_recv, loc, ssend, srecv, xsend, xrecv,
):
    x, y, z, r = place()
    width = tok_ref.shape[0]
    rows = tok_ref.shape[1]
    one = 1 - r
    c1 = x * one + z * r
    c2 = z * one + x * r

    def along1(by):
        return device(step(x, by * one), y, step(z, by * r), r)

    def along2(by):
        return device(step(x, by * r), y, step(z, by * one), r)

    def along_y(by):
        return device(x, step(y, by), z, r)

    sibling = device(x, y, z, 1 - r)
    greet([along1(1), along1(-1), along2(1), along2(-1),
           along_y(1), along_y(-1), along_y(2), sibling])

    sent = []

    def go(*args):
        copy = send(*args)
        sent.append(copy)
        return copy

    local = []
    for ph in range(2):
        kind = 2 * ph + r
        copy = pltpu.make_async_copy(wcat_ref.at[kind], wbuf.at[kind, c2, c1], loc.at[ph])
        copy.start()
        local.append(copy)

    def stage1a(ph):
        kind = 2 * ph + r
        src, dst = wcat_ref.at[kind], wbuf.at[kind, c2, c1]
        return [go(src, dst, wsend.at[ph, i], wrecv.at[ph, i], along1(by))
                for i, by in enumerate((1, -1))]

    def stage1b(ph, before):
        kind = 2 * ph + r
        half = wbuf.shape[4] // 2
        out = []
        for i, by in enumerate((1, -1)):
            before[i].wait_recv()
            ref = wbuf.at[kind, c2, step(c1, -by), :, pl.ds(i * half, half)]
            out.append(go(ref, ref, wsend.at[ph, 2 + i], wrecv.at[ph, 2 + i], along1(by)))
        return out

    def to_sibling(ph, i, row):
        ref = wbuf.at[2 * ph + r, row]
        return go(ref, ref, sib_send.at[ph, i], sib_recv.at[ph, i], sibling)

    def stage2a(ph, before):
        kind = 2 * ph + r
        local[ph].wait()
        for copy in before:
            copy.wait_recv()
        ref = wbuf.at[kind, c2]
        out = [go(ref, ref, wsend.at[ph, 4 + i], wrecv.at[ph, 4 + i], along2(by))
               for i, by in enumerate((1, -1))]
        return out, [to_sibling(ph, 0, c2)]

    def stage2b(ph, before, sib):
        kind = 2 * ph + r
        out = []
        for i, by in enumerate((1, -1)):
            before[i].wait_recv()
            row = step(c2, -by)
            ref = wbuf.at[kind, row, pl.ds(2 * i, 2)]
            out.append(go(ref, ref, wsend.at[ph, 6 + i], wrecv.at[ph, 6 + i], along2(by)))
        for i, by in enumerate((1, -1)):
            sib.append(to_sibling(ph, 1 + i, step(c2, -by)))
        return out

    def stage2c(ph, before, sib):
        for copy in before:
            copy.wait_recv()
        sib.append(to_sibling(ph, 3, step(c2, 2)))

    a0 = stage1a(0)

    raw = tok_ref[...].astype(F32)
    sums[y] = jnp.sum(raw * raw, axis=0, keepdims=True)
    told = [go(sums.at[y], sums.at[y], ssend.at[i], srecv.at[i], along_y(by))
            for i, by in enumerate((1, 2, 3))]
    for copy in told:
        copy.wait_recv()
    total = sums[0] + sums[1] + sums[2] + sums[3]
    scale = lax.rsqrt(total * (1.0 / (RING * width)) + 1e-06)

    def norm_chunk(at, size):
        part = tok_ref[pl.ds(at, size), :].astype(F32)
        part = part * scale * gain_ref[pl.ds(at, size), :]
        xbuf[y, :, pl.ds(at, size)] = part.T.astype(BF16)

    lanes = 128

    def norm_step(i, carry):
        norm_chunk(pl.multiple_of(i * lanes, lanes), lanes)
        return carry

    lax.fori_loop(0, width // lanes, norm_step, 0)
    if width % lanes:
        norm_chunk(width // lanes * lanes, width % lanes)
    xa = [go(xbuf.at[y], xbuf.at[y], xsend.at[i], xrecv.at[i], along_y(by))
          for i, by in enumerate((1, -1))]

    b0 = stage1b(0, a0)
    d0, sib0 = stage2a(0, b0)
    a1 = stage1a(1)
    b1 = stage1b(1, a1)
    e0 = stage2b(0, d0, sib0)
    d1, sib1 = stage2a(1, b1)
    xb = []
    for i, by in enumerate((1, -1)):
        xa[i].wait_recv()
        ref = xbuf.at[step(y, -by), pl.ds(i * (rows // 2), rows // 2)]
        xb.append(go(ref, ref, xsend.at[2 + i], xrecv.at[2 + i], along_y(by)))
    stage2c(0, e0, sib0)

    def multiply(ph, h, first):
        left = xbuf[h]
        for j in range(2):
            kind = 2 * ph + j
            block = wbuf[kind, h] if j == 0 else wbuf[kind, :, h]
            part = jnp.dot(left, block.reshape(width, block.shape[2]), preferred_element_type=F32)
            if first:
                acc[kind] = part
            else:
                acc[kind] += part

    for copy in sib0:
        copy.wait_recv()
    multiply(0, y, True)
    e1 = stage2b(1, d1, sib1)
    lax.fori_loop(0, 2, lambda i, c: (multiply(0, step(y, 1 + 2 * i), False), c)[1], 0)
    for copy in xb:
        copy.wait_recv()
    multiply(0, step(y, 2), False)

    cosine, sine = cos_ref[...], sin_ref[...]

    def turn(u, gain):
        u = u * lax.rsqrt(jnp.mean(u * u, axis=-1, keepdims=True) + 1e-06) * gain
        return u * cosine + pltpu.roll(u, HEAD_WIDTH // 2, 1) * sine

    key_gain, query_gain = kg_ref[...], qg_ref[...]
    for head in range(4):
        cols = pl.ds(head * HEAD_WIDTH, HEAD_WIDTH)
        k_ref[:, cols] = turn(acc[0, :, cols], key_gain).astype(BF16)
    v_ref[...] = acc[1].astype(BF16)

    stage2c(1, e1, sib1)
    for copy in sib1:
        copy.wait_recv()
    multiply(1, y, True)
    lax.fori_loop(1, RING, lambda i, c: (multiply(1, step(y, i), False), c)[1], 0)
    for kind in range(2):
        for head in range(4):
            cols = pl.ds(head * HEAD_WIDTH, HEAD_WIDTH)
            dest = pl.ds((kind * 4 + head) * HEAD_WIDTH, HEAD_WIDTH)
            turned = turn(acc[2 + kind, :, cols], query_gain) * QSCALE ** (-0.5)
            q_ref[:, dest] = turned.astype(BF16)
    for copy in sent:
        copy.wait_send()


def project(tok, gain, wcat, query_gain, key_gain, cosine, sine):
    width, rows = tok.shape
    depth, cols = wcat.shape[1:]
    dma = pltpu.SemaphoreType.DMA
    vmem = pl.BlockSpec(memory_space=pltpu.VMEM)
    return pl.pallas_call(
        project_kernel,
        out_shape=(
            jax.ShapeDtypeStruct((rows, 2 * cols), BF16),
            jax.ShapeDtypeStruct((rows, cols), BF16),
            jax.ShapeDtypeStruct((rows, cols), BF16),
        ),
        in_specs=[vmem, vmem, pl.BlockSpec(memory_space=pl.ANY), vmem, vmem, vmem, vmem],
        out_specs=(vmem, vmem, vmem),
        scratch_shapes=[
            pltpu.VMEM((4, RING, RING, depth, cols), BF16),
            pltpu.VMEM((RING, rows, width), BF16),
            pltpu.VMEM((4, rows, cols), F32),
            pltpu.VMEM((RING, 1, rows), F32),
            dma((2, 8)), dma((2, 8)), dma((2, 4)), dma((2, 4)), dma((2,)),
            dma((3,)), dma((3,)), dma((4,)), dma((4,)),
        ],
        compiler_params=pltpu.CompilerParams(
            collective_id=0, has_side_effects=True, vmem_limit_bytes=58 * 2**20
        ),
        cost_estimate=pl.CostEstimate(
            flops=2 * rows * RING * width * 4 * cols, bytes_accessed=10**8, transcendentals=0
        ),
    )(tok, gain, wcat, query_gain, key_gain, cosine, sine)


def shifted(x, axis, by):
    count = lax.axis_size(axis)
    pairs = [(i, i + by) for i in range(count) if 0 <= i + by < count]
    return lax.ppermute(x, axis, pairs)


def shards(tokens, norm_gain, w_query, w_key, w_value, query_gain, key_gain, w_out):
    rows, width = tokens.shape
    hid = lax.axis_index("hid")
    gain = lax.dynamic_slice_in_dim(norm_gain, hid * width, width).reshape(width, 1)
    cols = w_key.shape[1]
    wcat = jnp.stack([w_key, w_value, w_query[:, :cols], w_query[:, cols:]])
    local_heads = w_query.shape[1] // HEAD_WIDTH
    local_kv = w_key.shape[1] // HEAD_WIDTH
    base = lax.axis_index("seq") * rows
    qpos = base + jnp.arange(rows, dtype=jnp.int32)
    half = HEAD_WIDTH // 2
    freq = 10000.0 ** (-(jnp.arange(half, dtype=F32) * 2.0) / HEAD_WIDTH)
    angle = qpos.astype(F32)[:, None] * freq[None, :]
    cosine, sine = jnp.cos(angle), jnp.sin(angle)
    qh, kh, value_head = project(
        tokens.T, gain, wcat,
        query_gain.reshape(1, -1), key_gain.reshape(1, -1),
        jnp.concatenate([cosine, cosine], axis=1), jnp.concatenate([-sine, sine], axis=1),
    )
    qh = qh.reshape(rows, local_heads, HEAD_WIDTH)
    kh = kh.reshape(rows, local_kv, HEAD_WIDTH)
    value_head = value_head.reshape(rows, local_kv, HEAD_WIDTH)
    key_blocks = []
    value_blocks = []
    for distance in range(1, DEPTH + 1):
        arrived = shifted((kh, value_head), "seq", distance)
        key_blocks.insert(0, arrived[0])
        value_blocks.insert(0, arrived[1])
    keys = jnp.concatenate(key_blocks + [kh], axis=0)
    values = jnp.concatenate(value_blocks + [value_head], axis=0)
    window_extent = keys.shape[0]
    kpos = base - DEPTH * rows + jnp.arange(window_extent, dtype=jnp.int32)
    diff = qpos[:, None] - kpos[None, :]
    allowed = (diff >= 0) & (diff < WINDOW) & (kpos >= 0)[None, :]
    group = local_heads // local_kv
    grouped = qh.reshape(rows, local_kv, group, HEAD_WIDTH).transpose(1, 0, 2, 3)

    def one_head(operands):
        qpart, kpart, vpart = operands
        scores = jnp.einsum("rgd,ld->grl", qpart, kpart, preferred_element_type=F32)
        scores = jnp.where(allowed[None], scores, -jnp.inf)
        probs = jax.nn.softmax(scores, axis=-1).astype(BF16)
        mixed = jnp.einsum("grl,ld->rgd", probs, vpart, preferred_element_type=F32)
        return mixed.astype(BF16)

    per_head = lax.map(one_head, (grouped, keys.transpose(1, 0, 2), values.transpose(1, 0, 2)))
    heads_out = per_head.transpose(1, 0, 2, 3).reshape(rows, local_heads * HEAD_WIDTH)
    terms = jnp.dot(
        heads_out,
        lax.all_gather(w_out, "seq", axis=1, tiled=True),
        preferred_element_type=F32,
    )
    return lax.psum_scatter(terms.astype(BF16), "hid", scatter_dimension=1, tiled=True)


def solution(mesh):
    return jax.shard_map(
        shards,
        mesh=mesh,
        in_specs=(
            P(("rep", "seq"), "hid"),
            P(),
            P("seq", "hid"),
            P("seq", "hid"),
            P("seq", "hid"),
            P(),
            P(),
            P("hid", "seq"),
        ),
        out_specs=P(("rep", "seq"), "hid"),
        check_vma=False,
    )
```

time: 467 us -> 325 us (0.70)
  waiting for transfers between devices: 337 us -> 88.9 us
  Pallas kernels: 0 us -> 136 us
  matrix products: 77.9 us -> 50.3 us
  other arithmetic: 18.1 us -> 11.7 us
  local copies, waits for them, and re-layouts: 2.44 us -> 7.25 us
    all_gather x4 -> x0, waiting for transfers between devices: 226 us -> none  [the longest x1 59.7 us: shards(): whole = lax.all_gather(tokens, 'hid', axis=1, tiled=True)]
    pallas_call x0 -> x1, Pallas kernels: none -> 136 us  [project(): pl.pallas_call(project_kernel, out_shape=(jax.ShapeDtypeStruct((rows, 2 *...]
    dot_general x7 -> x4, matrix products: 42.9 us -> 16.9 us  [one_head(): mixed = jnp.einsum('grl,ld->rgd', probs, vpart, preferred_element_type=F32)]
    all_gather x1, waiting for transfers between devices: 23.9 us -> 0.01 us  [shards(): lax.all_gather(w_out, 'seq', axis=1, tiled=True)]
  transfers between devices with their start and end apart: 10 -> 6, of which waited for: 8 -> 4; matrix products, arithmetic and copies ran while one was open for 18% -> 18% of each run, Pallas kernels for 0% -> 42%
where the time goes in v1:
time: 325 us; the launch traced here: 323 us
  Pallas kernels  136 us (42%)
  waiting for transfers between devices  88.9 us (27%)
  matrix products  50.3 us (15%)
  starting transfers between devices  15.2 us (5%)
  between operations  13.5 us (4%)
  other arithmetic  11.7 us (4%)
  local copies, waits for them, and re-layouts  7.25 us (2%)
    pallas_call x1, Pallas kernels, project(): pl.pallas_call(project_kernel, out_shape=(jax.ShapeDtypeStruct((rows, 2 *...  136 us
    reduce_scatter x1, waiting for transfers between devices, shards(): lax.psum_scatter(terms.astype(BF16), 'hid', scatter_dimension=1, tiled=True)  59.1 us
    ppermute x4, waiting for transfers between devices, shifted(): return lax.ppermute(x, axis, pairs)  29.1 us
    sub x4, matrix products, one_head(): probs = jax.nn.softmax(scores, axis=-1).astype(BF16)  23 us
    dot_general x4, matrix products, one_head(): mixed = jnp.einsum('grl,ld->rgd', probs, vpart, preferred_element_type=F32)  16.9 us
    ppermute x4, starting transfers between devices, shifted(): return lax.ppermute(x, axis, pairs)  15.1 us
    dot_general x1, matrix products, shards(): jnp.dot(heads_out, lax.all_gather(w_out, 'seq', axis=1, tiled=True), pref...  10.4 us
  transfers between devices with their start and end apart: 6, of which 4 were waited for; matrix products, arithmetic and copies ran while one was open for 18% of the time, Pallas kernels for 42%

profile of v1, /device:TPU:0, one launch (start us, length us, event | category | flops | bytes accessed | tf_op | source)
XLA Modules:
  0.0 323.1 jit_solution(11798845705234396355)
XLA Ops:
  8.1 1.1 reshape.50.gain_ref
  10.2 1.0 pad_maximum_fusion.1
  11.3 1.3 pad_maximum_fusion.wcat_ref
  12.6 136.3 %shard_map.82 = (bf16[512,1024]{1,0:T(8,128)(2,1)}, bf16[512,512]{1,0:T(8,128)(2,1)}, bf16[512,512]{1,0:T(8,128)(2,1)}) custom-call(bf16[1344,512]{1,0:T(8,128)(2,1)} %bitcast.89, f32[1344,1]{1,0:T(8,128)} %reshape.50.gain_ref, bf16[4,336,512]{2,1,0:T(8,128)(2,1)} %pad_maximum_fusion.wcat_ref, f32[1,128]{1,0:T(1,128)} %bitcast.90, f32[1,128]{1,0:T(1,128)} %bitcast.91, ...), custom_call_target="tpu_custom_call" | custom-call | flops 11274289152 | bytes 100000000 | tf_op jit(solution)/shard_map/pallas_call | solution.py:233
  148.9 1.1 copy_bitcast_fusion.1
  150.0 4.1 %collective-permute-start.2 = (bf16[512,4,128]{2,0,1:T(8,128)(2,1)S(1)}, bf16[512,4,128]{2,0,1:T(8,128)(2,1)S(1)}, u32[]{:S(2)}, u32[]{:S(2)}) collective-permute-start(bf16[512,4,128]{2,0,1:T(8,128)(2,1)S(1)} %copy_bitcast_fusion.1), channel_id=1, source_target_pairs={{0,16},{8,24},{16,32},{24,40},{32,48},{40,56},{48,64},{56,72},{64,... | collective-permute-start | bytes 1572872 | tf_op jit(solution)/shard_map/ppermute | solution.py:262
  154.1 3.7 %collective-permute-start.3 = (bf16[512,4,128]{2,0,1:T(8,128)(2,1)S(1)}, bf16[512,4,128]{2,0,1:T(8,128)(2,1)}, u32[]{:S(2)}, u32[]{:S(2)}) collective-permute-start(bf16[512,4,128]{2,0,1:T(8,128)(2,1)S(1)} %copy_bitcast_fusion.1), channel_id=1, source_target_pairs={{0,8},{8,16},{16,24},{24,32},{32,40},{40,48},{48,56},{56,64},{64,7... | collective-permute-start | bytes 1572872 | tf_op jit(solution)/shard_map/ppermute | solution.py:262
  157.8 1.3 copy.27
  159.0 4.1 %collective-permute-start = (bf16[512,4,128]{0,2,1:T(8,128)(2,1)S(1)}, bf16[512,4,128]{0,2,1:T(8,128)(2,1)}, u32[]{:S(2)}, u32[]{:S(2)}) collective-permute-start(bf16[512,4,128]{0,2,1:T(8,128)(2,1)S(1)} %bitcast.83), channel_id=1, source_target_pairs={{0,16},{8,24},{16,32},{24,40},{32,48},{40,56},{48,64},{56,72},{64,... | collective-permute-start | bytes 1572872 | tf_op jit(solution)/shard_map/ppermute | solution.py:262
  163.2 3.3 %collective-permute-start.1 = (bf16[512,4,128]{0,2,1:T(8,128)(2,1)S(1)}, bf16[512,4,128]{0,2,1:T(8,128)(2,1)}, u32[]{:S(2)}, u32[]{:S(2)}) collective-permute-start(bf16[512,4,128]{0,2,1:T(8,128)(2,1)S(1)} %bitcast.84), channel_id=1, source_target_pairs={{0,8},{8,16},{16,24},{24,32},{32,40},{40,48},{48,56},{56,64},{64,7... | collective-permute-start | bytes 1572872 | tf_op jit(solution)/shard_map/ppermute | solution.py:262
  166.4 1.8 reshape_reshape.3
  168.2 1.1 copy.31
  169.4 7.7 %collective-permute-done.3 = bf16[512,4,128]{2,0,1:T(8,128)(2,1)} collective-permute-done((bf16[512,4,128]{2,0,1:T(8,128)(2,1)S(1)}, bf16[512,4,128]{2,0,1:T(8,128)(2,1)}, u32[]{:S(2)}, u32[]{:S(2)}) %collective-permute-start.3) | collective-permute-done | bytes 524320 | tf_op jit(solution)/shard_map/ppermute | solution.py:262
  177.1 1.1 maximum_bitcast_fusion.1
  178.2 10.1 %collective-permute-done = bf16[512,4,128]{0,2,1:T(8,128)(2,1)} collective-permute-done((bf16[512,4,128]{0,2,1:T(8,128)(2,1)S(1)}, bf16[512,4,128]{0,2,1:T(8,128)(2,1)}, u32[]{:S(2)}, u32[]{:S(2)}) %collective-permute-start) | collective-permute-done | bytes 524320 | tf_op jit(solution)/shard_map/ppermute | solution.py:262
  188.4 11.2 %collective-permute-done.1 = bf16[512,4,128]{0,2,1:T(8,128)(2,1)} collective-permute-done((bf16[512,4,128]{0,2,1:T(8,128)(2,1)S(1)}, bf16[512,4,128]{0,2,1:T(8,128)(2,1)}, u32[]{:S(2)}, u32[]{:S(2)}) %collective-permute-start.1) | collective-permute-done | bytes 524320 | tf_op jit(solution)/shard_map/ppermute | solution.py:262
  199.6 2.5 maximum_bitcast_fusion
  202.1 44.6 %while.11 = (s32[]{:T(128)}, bf16[4,512,2,128]{1,3,2,0:T(8,128)(2,1)}, bf16[4,1536,128]{1,2,0:T(8,128)(2,1)}, bf16[4,1536,128]{2,1,0:T(8,128)(2,1)S(1)}, bf16[4,...) while((s32[]{:T(128)}, ...), condition=%wide.region_3.4_spmd.clone, body=%wide.region_0.3_spmd.clone.sunk | while | flops 817235456 | bytes 15486557 | solution.py:310
  202.1 1.2 fusion.64
  203.3 5.7 %fusion.65 = (f32[2,512]{1,0:T(2,128)S(1)}, f32[2,512,1536]{1,2,0:T(8,128)}) fusion(pred[512,1536]{0,1:T(8,128)(4,1)S(1)} %fusion.64, bf16[4,1536,128]{2,1,0:T(8,128)(2,1)S(1)} %get-tuple-element.164, s32[]{:T(128)} %get-tuple-element.152, bf16[4,512,2,128]{3,1,2,0:T(8,128)(2,1)} %get-tuple-element.165), kind=kOutput, calls=%fused_computation.50.clone.1 | convolution fusion | flops 407373312 | bytes 7738368 | tf_op jit(solution)/shard_map/while/body/eval_jaxpr/sub | solution.py:306
  209.0 4.2 %fusion.66 = bf16[4,512,2,128]{1,3,2,0:T(8,128)(2,1)} fusion(bf16[4,512,2,128]{1,3,2,0:T(8,128)(2,1)} %get-tuple-element.153, s32[]{:T(128)} %get-tuple-element.152, f32[2,512,1536]{1,2,0:T(8,128)} %get-tuple-element.141, f32[2,512]{1,0:T(2,128)S(1)} %get-tuple-element.142, bf16[4,1536,128]{1,2,0:T(8,128)(2,1)} %get-tuple-element.163), kind=kOutput, calls=%fused_computation.15.clone.1 | convolution fusion | flops 405929984 | bytes 6951936 | tf_op jit(solution)/shard_map/while/body/eval_jaxpr/grl,ld->rgd/dot_general | solution.py:307
  213.2 1.2 fusion.64
  214.4 5.7 %fusion.65 = (f32[2,512]{1,0:T(2,128)S(1)}, f32[2,512,1536]{1,2,0:T(8,128)}) fusion(pred[512,1536]{0,1:T(8,128)(4,1)S(1)} %fusion.64, bf16[4,1536,128]{2,1,0:T(8,128)(2,1)S(1)} %get-tuple-element.164, s32[]{:T(128)} %get-tuple-element.152, bf16[4,512,2,128]{3,1,2,0:T(8,128)(2,1)} %get-tuple-element.165), kind=kOutput, calls=%fused_computation.50.clone.1 | convolution fusion | flops 407373312 | bytes 7738368 | tf_op jit(solution)/shard_map/while/body/eval_jaxpr/sub | solution.py:306
  220.2 4.2 %fusion.66 = bf16[4,512,2,128]{1,3,2,0:T(8,128)(2,1)} fusion(bf16[4,512,2,128]{1,3,2,0:T(8,128)(2,1)} %get-tuple-element.153, s32[]{:T(128)} %get-tuple-element.152, f32[2,512,1536]{1,2,0:T(8,128)} %get-tuple-element.141, f32[2,512]{1,0:T(2,128)S(1)} %get-tuple-element.142, bf16[4,1536,128]{1,2,0:T(8,128)(2,1)} %get-tuple-element.163), kind=kOutput, calls=%fused_computation.15.clone.1 | convolution fusion | flops 405929984 | bytes 6951936 | tf_op jit(solution)/shard_map/while/body/eval_jaxpr/grl,ld->rgd/dot_general | solution.py:307
  224.4 1.2 fusion.64
  225.6 5.7 %fusion.65 = (f32[2,512]{1,0:T(2,128)S(1)}, f32[2,512,1536]{1,2,0:T(8,128)}) fusion(pred[512,1536]{0,1:T(8,128)(4,1)S(1)} %fusion.64, bf16[4,1536,128]{2,1,0:T(8,128)(2,1)S(1)} %get-tuple-element.164, s32[]{:T(128)} %get-tuple-element.152, bf16[4,512,2,128]{3,1,2,0:T(8,128)(2,1)} %get-tuple-element.165), kind=kOutput, calls=%fused_computation.50.clone.1 | convolution fusion | flops 407373312 | bytes 7738368 | tf_op jit(solution)/shard_map/while/body/eval_jaxpr/sub | solution.py:306
  231.3 4.2 %fusion.66 = bf16[4,512,2,128]{1,3,2,0:T(8,128)(2,1)} fusion(bf16[4,512,2,128]{1,3,2,0:T(8,128)(2,1)} %get-tuple-element.153, s32[]{:T(128)} %get-tuple-element.152, f32[2,512,1536]{1,2,0:T(8,128)} %get-tuple-element.141, f32[2,512]{1,0:T(2,128)S(1)} %get-tuple-element.142, bf16[4,1536,128]{1,2,0:T(8,128)(2,1)} %get-tuple-element.163), kind=kOutput, calls=%fused_computation.15.clone.1 | convolution fusion | flops 405929984 | bytes 6951936 | tf_op jit(solution)/shard_map/while/body/eval_jaxpr/grl,ld->rgd/dot_general | solution.py:307
  235.6 1.2 fusion.64
  236.8 5.7 %fusion.65 = (f32[2,512]{1,0:T(2,128)S(1)}, f32[2,512,1536]{1,2,0:T(8,128)}) fusion(pred[512,1536]{0,1:T(8,128)(4,1)S(1)} %fusion.64, bf16[4,1536,128]{2,1,0:T(8,128)(2,1)S(1)} %get-tuple-element.164, s32[]{:T(128)} %get-tuple-element.152, bf16[4,512,2,128]{3,1,2,0:T(8,128)(2,1)} %get-tuple-element.165), kind=kOutput, calls=%fused_computation.50.clone.1 | convolution fusion | flops 407373312 | bytes 7738368 | tf_op jit(solution)/shard_map/while/body/eval_jaxpr/sub | solution.py:306
  242.5 4.2 %fusion.66 = bf16[4,512,2,128]{1,3,2,0:T(8,128)(2,1)} fusion(bf16[4,512,2,128]{1,3,2,0:T(8,128)(2,1)} %get-tuple-element.153, s32[]{:T(128)} %get-tuple-element.152, f32[2,512,1536]{1,2,0:T(8,128)} %get-tuple-element.141, f32[2,512]{1,0:T(2,128)S(1)} %get-tuple-element.142, bf16[4,1536,128]{1,2,0:T(8,128)(2,1)} %get-tuple-element.163), kind=kOutput, calls=%fused_computation.15.clone.1 | convolution fusion | flops 405929984 | bytes 6951936 | tf_op jit(solution)/shard_map/while/body/eval_jaxpr/grl,ld->rgd/dot_general | solution.py:307
  246.7 10.4 %convolution_convert_fusion = bf16[512,5376]{0,1:T(8,128)(2,1)} fusion(bf16[1024,5376]{0,1:T(8,128)(2,1)} %all-gather.2.cloned.1.call-done, bf16[512,1024]{0,1:T(8,128)(2,1)} %bitcast.92), kind=kOutput, calls=%fused_computation.32 | convolution fusion | flops 5639897088 | bytes 17563648 | tf_op jit(solution)/shard_map/dot_general | solution.py:312
  257.2 59.1 %reduce-scatter.2.cloned.1.call-done = bf16[512,1344]{0,1:T(8,128)(2,1)} async-done(((bf16[512,5376]{0,1:T(8,128)(2,1)}), bf16[512,1344]{0,1:T(8,128)(2,1)}) %reduce-scatter.2.cloned.1.call-update) | async-done | bytes 1376272 | tf_op jit(solution)/shard_map/reduce_scatter | solution.py:317
  (21 shorter events, 2.6 us)
Async XLA Ops:
  6.5 4.7 %copy-start = (bf16[336,1024]{1,0:T(8,128)(2,1)S(1)}, bf16[336,1024]{1,0:T(8,128)(2,1)}, u32[]{:S(2)}) copy-start(bf16[336,1024]{1,0:T(8,128)(2,1)} %param.12) | copy-start | bytes 2064388
  6.5 4.8 %copy-start.2 = (bf16[336,512]{1,0:T(8,128)(2,1)S(1)}, bf16[336,512]{1,0:T(8,128)(2,1)}, u32[]{:S(2)}) copy-start(bf16[336,512]{1,0:T(8,128)(2,1)} %param.13) | copy-start | bytes 1032196
  6.5 4.8 %copy-start.1 = (bf16[336,512]{1,0:T(8,128)(2,1)S(1)}, bf16[336,512]{1,0:T(8,128)(2,1)}, u32[]{:S(2)}) copy-start(bf16[336,512]{1,0:T(8,128)(2,1)} %param.14) | copy-start | bytes 1032196
  6.5 240.2 %all-gather.2.cloned.1.call-start = ((), (), s32[]{:S(2)}) async-start(), calls=%async_computation.1 | async-start | bytes 11698176 | tf_op jit(solution)/shard_map/all_gather | solution.py:314
  7.3 309.0 %reduce-scatter.2.cloned.1.call-start = ((), (), s32[]{:S(2)}) async-start(), calls=%async_computation.2 | async-start | bytes 6881280 | tf_op jit(solution)/shard_map/reduce_scatter | solution.py:317
  150.0 19.4 %collective-permute-start.2 = (bf16[512,4,128]{2,0,1:T(8,128)(2,1)S(1)}, bf16[512,4,128]{2,0,1:T(8,128)(2,1)S(1)}, u32[]{:S(2)}, u32[]{:S(2)}) collective-permute-start(bf16[512,4,128]{2,0,1:T(8,128)(2,1)S(1)} %copy_bitcast_fusion.1), channel_id=1, source_target_pairs={{0,16},{8,24},{16,32},{24,40},{32,48},{40,56},{48,64},{56,72},{64,... | collective-permute-start | bytes 1572872 | tf_op jit(solution)/shard_map/ppermute | solution.py:262
  154.1 23.0 %collective-permute-start.3 = (bf16[512,4,128]{2,0,1:T(8,128)(2,1)S(1)}, bf16[512,4,128]{2,0,1:T(8,128)(2,1)}, u32[]{:S(2)}, u32[]{:S(2)}) collective-permute-start(bf16[512,4,128]{2,0,1:T(8,128)(2,1)S(1)} %copy_bitcast_fusion.1), channel_id=1, source_target_pairs={{0,8},{8,16},{16,24},{24,32},{32,40},{40,48},{48,56},{56,64},{64,7... | collective-permute-start | bytes 1572872 | tf_op jit(solution)/shard_map/ppermute | solution.py:262
  159.0 29.3 %collective-permute-start = (bf16[512,4,128]{0,2,1:T(8,128)(2,1)S(1)}, bf16[512,4,128]{0,2,1:T(8,128)(2,1)}, u32[]{:S(2)}, u32[]{:S(2)}) collective-permute-start(bf16[512,4,128]{0,2,1:T(8,128)(2,1)S(1)} %bitcast.83), channel_id=1, source_target_pairs={{0,16},{8,24},{16,32},{24,40},{32,48},{40,56},{48,64},{56,72},{64,... | collective-permute-start | bytes 1572872 | tf_op jit(solution)/shard_map/ppermute | solution.py:262
  163.2 36.4 %collective-permute-start.1 = (bf16[512,4,128]{0,2,1:T(8,128)(2,1)S(1)}, bf16[512,4,128]{0,2,1:T(8,128)(2,1)}, u32[]{:S(2)}, u32[]{:S(2)}) collective-permute-start(bf16[512,4,128]{0,2,1:T(8,128)(2,1)S(1)} %bitcast.84), channel_id=1, source_target_pairs={{0,8},{8,16},{16,24},{24,32},{32,40},{40,48},{48,56},{56,64},{64,7... | collective-permute-start | bytes 1572872 | tf_op jit(solution)/shard_map/ppermute | solution.py:262
Sparse Core Ops, SparseCore 0:
  9.5 112.0 all-gather.1
  257.3 58.9 reduce-scatter.1

commit v2 on v1

--- a/solution.py
+++ b/solution.py
@@ -12,6 +12,7 @@
 QSCALE = 168
 DEPTH = 2
 RING = 4
+QB = 128
 MESH = pl.DeviceIdType.MESH
 BF16 = jnp.bfloat16
 F32 = jnp.float32
@@ -256,10 +257,198 @@
     )(tok, gain, wcat, query_gain, key_gain, cosine, sine)
 
 
-def shifted(x, axis, by):
-    count = lax.axis_size(axis)
-    pairs = [(i, i + by) for i in range(count) if 0 <= i + by < count]
-    return lax.ppermute(x, axis, pairs)
+def attend_kernel(
+    q_ref, k_ref, v_ref, wo_ref,
+    out_ref,
+    wbuf, kbuf, vbuf, relay, heads, sbuf, rhalf, rfull,
+    wsend, wrecv, sib_send, sib_recv, loc, hsend, hrecv, rsend, rrecv,
+):
+    x, y, z, r = place()
+    rows = q_ref.shape[0]
+    count = RING * RING
+    seq = z * RING + x
+    one = 1 - r
+    c1 = x * one + z * r
+    c2 = z * one + x * r
+
+    def along1(by):
+        return device(step(x, by * one), y, step(z, by * r), r)
+
+    def along2(by):
+        return device(step(x, by * r), y, step(z, by * one), r)
+
+    def along_y(by):
+        return device(x, step(y, by), z, r)
+
+    def at_seq(s):
+        return {"seq": s, "hid": y, "rep": r}
+
+    def around(s):
+        return lax.rem(s + count, count)
+
+    sibling = device(x, y, z, 1 - r)
+    after = at_seq(around(seq + 1))
+    before = at_seq(around(seq - 1))
+    via = device(step(x, -1), y, z, r)
+    via_from = device(step(x, 1), y, z, r)
+    onward = at_seq(around(z * RING + step(x, 1) + 2))
+    origin = around(seq - 2)
+    onward_from = device(step(lax.rem(origin, RING), -1), y, lax.div(origin, RING), r)
+    greet([along1(1), along1(-1), along2(1), along2(-1), along_y(1), along_y(-1),
+           sibling, after, before, via, via_from, onward, onward_from])
+
+    sent = []
+
+    def go(*args):
+        copy = send(*args)
+        sent.append(copy)
+        return copy
+
+    def slot(i):
+        return pl.ds(i * rows, rows)
+
+    h0 = go(k_ref, kbuf.at[slot(1)], hsend.at[0], hrecv.at[0], after)
+    h1 = go(v_ref, vbuf.at[slot(1)], hsend.at[1], hrecv.at[1], after)
+    h2 = go(v_ref, relay, hsend.at[2], hrecv.at[2], via)
+
+    own = pltpu.make_async_copy(wo_ref.at[r], wbuf.at[r, c2, c1], loc)
+    own.start()
+    a = [go(wo_ref.at[r], wbuf.at[r, c2, c1], wsend.at[i], wrecv.at[i], along1(by))
+         for i, by in enumerate((1, -1))]
+    kbuf[slot(2)] = k_ref[...]
+    vbuf[slot(2)] = v_ref[...]
+    half = wbuf.shape[4] // 2
+    b = []
+    for i, by in enumerate((1, -1)):
+        a[i].wait_recv()
+        ref = wbuf.at[r, c2, step(c1, -by), :, pl.ds(i * half, half)]
+        b.append(go(ref, ref, wsend.at[2 + i], wrecv.at[2 + i], along1(by)))
+    own.wait()
+    for copy in b:
+        copy.wait_recv()
+
+    def to_sibling(i, row):
+        ref = wbuf.at[r, row]
+        return go(ref, ref, sib_send.at[i], sib_recv.at[i], sibling)
+
+    ref = wbuf.at[r, c2]
+    d = [go(ref, ref, wsend.at[4 + i], wrecv.at[4 + i], along2(by))
+         for i, by in enumerate((1, -1))]
+    sib = [to_sibling(0, c2)]
+    h0.wait_recv()
+    h3 = go(kbuf.at[slot(1)], kbuf.at[slot(0)], hsend.at[3], hrecv.at[3], after)
+    h2.wait_recv()
+    h4 = go(relay, vbuf.at[slot(0)], hsend.at[4], hrecv.at[4], onward)
+    e = []
+    for i, by in enumerate((1, -1)):
+        d[i].wait_recv()
+        ref = wbuf.at[r, step(c2, -by), pl.ds(2 * i, 2)]
+        e.append(go(ref, ref, wsend.at[6 + i], wrecv.at[6 + i], along2(by)))
+    for i, by in enumerate((1, -1)):
+        sib.append(to_sibling(1 + i, step(c2, -by)))
+    for copy in e:
+        copy.wait_recv()
+    sib.append(to_sibling(3, step(c2, 2)))
+
+    for copy in (h1, h3, h4):
+        copy.wait_recv()
+    span = WINDOW + QB
+    ri = lax.broadcasted_iota(jnp.int32, (QB, QB), 0)
+    ci = lax.broadcasted_iota(jnp.int32, (QB, QB), 1)
+    recent = jnp.concatenate([ci <= ri] * 2, axis=0)
+    oldest = jnp.concatenate([ci > ri] * 2, axis=0)
+    lane = lax.broadcasted_iota(jnp.int32, (1, span), 1)
+
+    def attend(it, carry):
+        g = lax.rem(it, RING)
+        i = lax.div(it, RING)
+        at = pl.multiple_of(i * QB, QB)
+        cols = pl.ds(pl.multiple_of(g * HEAD_WIDTH, HEAD_WIDTH), HEAD_WIDTH)
+        pair = [pl.ds(pl.multiple_of((2 * g + j) * HEAD_WIDTH, HEAD_WIDTH), HEAD_WIDTH)
+                for j in range(2)]
+        q = jnp.concatenate([q_ref[pl.ds(at, QB), c] for c in pair], axis=0)
+        k = kbuf[pl.ds(at, span), cols]
+        v = vbuf[pl.ds(at, span), cols]
+        s = lax.dot_general(q, k, (((1,), (1,)), ((), ())), preferred_element_type=F32)
+        present = lane + at >= DEPTH * rows - seq * rows
+        s = jnp.concatenate([
+            jnp.where(oldest, s[:, :QB], -jnp.inf), s[:, QB:WINDOW],
+            jnp.where(recent, s[:, WINDOW:], -jnp.inf)], axis=1)
+        s = jnp.where(present, s, -jnp.inf)
+        p = jnp.exp(s - jnp.max(s, axis=1, keepdims=True))
+        p = (p * (1.0 / jnp.sum(p, axis=1, keepdims=True))).astype(BF16)
+        o = jnp.dot(p, v, preferred_element_type=F32).astype(BF16)
+        for j in range(2):
+            heads[pl.ds(at, QB), pair[j]] = o[j * QB:(j + 1) * QB]
+        return carry
+
+    lax.fori_loop(0, RING * (rows // QB), attend, 0)
+    for copy in sib:
+        copy.wait_recv()
+
+    depth = wbuf.shape[3]
+    wide = wbuf.shape[4]
+
+    def terms(i, t):
+        def one_piece(j, carry):
+            part = lax.dot_general(wbuf[0, t, j], heads[:, :wide], (((1,), (1,)), ((), ())),
+                                   preferred_element_type=F32)
+            part += lax.dot_general(wbuf[1, j, t], heads[:, wide:], (((1,), (1,)), ((), ())),
+                                    preferred_element_type=F32)
+            sbuf[i, pl.ds(pl.multiple_of(j * depth, 16), depth), :] = part.astype(BF16)
+            return carry
+
+        lax.fori_loop(0, RING, one_piece, 0)
+
+    mid = RING * depth // 2
+    low, high = pl.ds(0, mid), pl.ds(mid, mid)
+    terms(0, step(y, 2))
+    f0 = go(sbuf.at[0, low], rhalf.at[0], rsend.at[0], rrecv.at[0], along_y(1))
+    f1 = go(sbuf.at[0, high], rhalf.at[1], rsend.at[1], rrecv.at[1], along_y(-1))
+    terms(1, step(y, 1))
+    g0 = go(sbuf.at[1, high], rfull.at[0, high], rsend.at[2], rrecv.at[2], along_y(1))
+    terms(2, step(y, -1))
+    g1 = go(sbuf.at[2, low], rfull.at[1, low], rsend.at[3], rrecv.at[3], along_y(-1))
+    terms(3, y)
+    f0.wait_recv()
+    sbuf[1, low, :] = (sbuf[1, low, :].astype(F32) + rhalf[0].astype(F32)).astype(BF16)
+    g2 = go(sbuf.at[1, low], rfull.at[0, low], rsend.at[4], rrecv.at[4], along_y(1))
+    f1.wait_recv()
+    sbuf[2, high, :] = (sbuf[2, high, :].astype(F32) + rhalf[1].astype(F32)).astype(BF16)
+    g3 = go(sbuf.at[2, high], rfull.at[1, high], rsend.at[5], rrecv.at[5], along_y(-1))
+    for copy in (g0, g1, g2, g3):
+        copy.wait_recv()
+    out_ref[...] = (sbuf[3].astype(F32) + rfull[0].astype(F32) + rfull[1].astype(F32)).astype(BF16)
+    for copy in sent:
+        copy.wait_send()
+
+
+def attend(qh, kh, vh, wo):
+    rows = qh.shape[0]
+    _, depth, cols = wo.shape
+    dma = pltpu.SemaphoreType.DMA
+    vmem = pl.BlockSpec(memory_space=pltpu.VMEM)
+    return pl.pallas_call(
+        attend_kernel,
+        out_shape=jax.ShapeDtypeStruct((RING * depth, rows), BF16),
+        in_specs=[vmem, vmem, vmem, pl.BlockSpec(memory_space=pl.ANY)],
+        out_specs=vmem,
+        scratch_shapes=[
+            pltpu.VMEM((2, RING, RING, depth, cols), BF16),
+            pltpu.VMEM((3 * rows, cols), BF16),
+            pltpu.VMEM((3 * rows, cols), BF16),
+            pltpu.VMEM((rows, cols), BF16),
+            pltpu.VMEM((rows, 2 * cols), BF16),
+            pltpu.VMEM((4, RING * depth, rows), BF16),
+            pltpu.VMEM((2, RING * depth // 2, rows), BF16),
+            pltpu.VMEM((2, RING * depth, rows), BF16),
+            dma((8,)), dma((8,)), dma((4,)), dma((4,)), dma,
+            dma((5,)), dma((5,)), dma((6,)), dma((6,)),
+        ],
+        compiler_params=pltpu.CompilerParams(
+            collective_id=1, has_side_effects=True, vmem_limit_bytes=58 * 2**20
+        ),
+    )(qh, kh, vh, wo)
 
 
 def shards(tokens, norm_gain, w_query, w_key, w_value, query_gain, key_gain, w_out):
@@ -268,8 +457,6 @@
     gain = lax.dynamic_slice_in_dim(norm_gain, hid * width, width).reshape(width, 1)
     cols = w_key.shape[1]
     wcat = jnp.stack([w_key, w_value, w_query[:, :cols], w_query[:, cols:]])
-    local_heads = w_query.shape[1] // HEAD_WIDTH
-    local_kv = w_key.shape[1] // HEAD_WIDTH
     base = lax.axis_index("seq") * rows
     qpos = base + jnp.arange(rows, dtype=jnp.int32)
     half = HEAD_WIDTH // 2
@@ -281,40 +468,9 @@
         query_gain.reshape(1, -1), key_gain.reshape(1, -1),
         jnp.concatenate([cosine, cosine], axis=1), jnp.concatenate([-sine, sine], axis=1),
     )
-    qh = qh.reshape(rows, local_heads, HEAD_WIDTH)
-    kh = kh.reshape(rows, local_kv, HEAD_WIDTH)
-    value_head = value_head.reshape(rows, local_kv, HEAD_WIDTH)
-    key_blocks = []
-    value_blocks = []
-    for distance in range(1, DEPTH + 1):
-        arrived = shifted((kh, value_head), "seq", distance)
-        key_blocks.insert(0, arrived[0])
-        value_blocks.insert(0, arrived[1])
-    keys = jnp.concatenate(key_blocks + [kh], axis=0)
-    values = jnp.concatenate(value_blocks + [value_head], axis=0)
-    window_extent = keys.shape[0]
-    kpos = base - DEPTH * rows + jnp.arange(window_extent, dtype=jnp.int32)
-    diff = qpos[:, None] - kpos[None, :]
-    allowed = (diff >= 0) & (diff < WINDOW) & (kpos >= 0)[None, :]
-    group = local_heads // local_kv
-    grouped = qh.reshape(rows, local_kv, group, HEAD_WIDTH).transpose(1, 0, 2, 3)
-
-    def one_head(operands):
-        qpart, kpart, vpart = operands
-        scores = jnp.einsum("rgd,ld->grl", qpart, kpart, preferred_element_type=F32)
-        scores = jnp.where(allowed[None], scores, -jnp.inf)
-        probs = jax.nn.softmax(scores, axis=-1).astype(BF16)
-        mixed = jnp.einsum("grl,ld->rgd", probs, vpart, preferred_element_type=F32)
-        return mixed.astype(BF16)
-
-    per_head = lax.map(one_head, (grouped, keys.transpose(1, 0, 2), values.transpose(1, 0, 2)))
-    heads_out = per_head.transpose(1, 0, 2, 3).reshape(rows, local_heads * HEAD_WIDTH)
-    terms = jnp.dot(
-        heads_out,
-        lax.all_gather(w_out, "seq", axis=1, tiled=True),
-        preferred_element_type=F32,
-    )
-    return lax.psum_scatter(terms.astype(BF16), "hid", scatter_dimension=1, tiled=True)
+    wo = w_out.T
+    wo = jnp.stack([wo[:, :cols], wo[:, cols:]])
+    return attend(qh, kh, value_head, wo).T
 
 
 def solution(mesh):

time: 325 us -> 238 us (0.73)
  Pallas kernels: 136 us -> 229 us
  waiting for transfers between devices: 88.9 us -> 0 us
  matrix products: 50.3 us -> 0 us
  starting transfers between devices: 15.2 us -> 0 us
  between operations: 13.5 us -> 0.07 us
  other arithmetic: 11.7 us -> 4.18 us
    pallas_call x0 -> x1, Pallas kernels: none -> 142 us  [attend(): pl.pallas_call(attend_kernel, out_shape=jax.ShapeDtypeStruct((RING * dept...]
    reduce_scatter x1 -> x0, waiting for transfers between devices: 59.1 us -> none  [shards(): lax.psum_scatter(terms.astype(BF16), 'hid', scatter_dimension=1, tiled=True)]
    pallas_call x1, Pallas kernels: 136 us -> 87.3 us  [project(): pl.pallas_call(project_kernel, out_shape=(jax.ShapeDtypeStruct((rows, 2 *...]
    ppermute x4 -> x0, waiting for transfers between devices: 29.1 us -> none  [shifted(): return lax.ppermute(x, axis, pairs)]
    dot_general x5 -> x0, matrix products: 27.3 us -> none  [the longest x4 16.9 us: one_head(): mixed = jnp.einsum('grl,ld->rgd', probs, vpart, preferred_element_type=F32)]
    sub x4 -> x0, matrix products: 23 us -> none  [one_head(): probs = jax.nn.softmax(scores, axis=-1).astype(BF16)]
    ppermute x4 -> x0, starting transfers between devices: 15.1 us -> none  [shifted(): return lax.ppermute(x, axis, pairs)]
    and x4 -> x0, other arithmetic: 4.75 us -> none  [shards(): allowed = (diff >= 0) & (diff < WINDOW) & (kpos >= 0)[None, :]]
  transfers between devices with their start and end apart: 6 -> 0, of which waited for: 4 -> 0; matrix products, arithmetic and copies ran while one was open for 18% -> 0% of each run, Pallas kernels for 42% -> 0%
where the time goes in v2:
time: 238 us
  Pallas kernels  229 us (96%)
  local copies, waits for them, and re-layouts  4.56 us (2%)
  other arithmetic  4.18 us (2%)
    pallas_call x1, Pallas kernels, attend(): pl.pallas_call(attend_kernel, out_shape=jax.ShapeDtypeStruct((RING * dept...  142 us
    pallas_call x1, Pallas kernels, project(): pl.pallas_call(project_kernel, out_shape=(jax.ShapeDtypeStruct((rows, 2 *...  87.3 us

profile of v2, /device:TPU:0, one launch (start us, length us, event | category | flops | bytes accessed | tf_op | source)
XLA Modules:
  0.0 237.7 jit_solution(10933972203555303914)
XLA Ops:
  0.0 0.0 copy-start
  0.0 1.0 fusion
  1.0 1.0 pad_maximum_fusion.2
  2.0 0.0 copy-start.2
  2.0 0.0 copy-start.3
  2.0 0.8 dynamic_slice.3
  2.9 1.1 reshape.24.gain_ref
  4.0 0.0 copy-done
  4.0 0.0 copy-done.2
  4.1 0.0 copy-done.3
  4.1 1.3 pad_maximum_fusion.wcat_ref
  5.3 0.0 copy-start.1
  5.3 87.3 %shard_map.82 = (bf16[512,1024]{1,0:T(8,128)(2,1)}, bf16[512,512]{1,0:T(8,128)(2,1)}, bf16[512,512]{1,0:T(8,128)(2,1)}) custom-call(bf16[1344,512]{1,0:T(8,128)(2,1)} %bitcast.19, f32[1344,1]{1,0:T(8,128)} %reshape.24.gain_ref, bf16[4,336,512]{2,1,0:T(8,128)(2,1)} %pad_maximum_fusion.wcat_ref, f32[1,128]{1,0:T(1,128)} %bitcast.20, f32[1,128]{1,0:T(1,128)} %bitcast.21, ...), custom_call_target="tpu_custom_call" | custom-call | flops 11274289152 | bytes 100000000 | tf_op jit(solution)/shard_map/pallas_call | solution.py:234
  92.6 0.0 copy-done.1
  92.7 0.9 pad_maximum_fusion.1.wo_ref
  93.6 141.6 %shard_map.83 = bf16[1344,512]{1,0:T(8,128)(2,1)} custom-call(bf16[512,1024]{1,0:T(8,128)(2,1)} %get-tuple-element.8.q_ref, bf16[512,512]{1,0:T(8,128)(2,1)} %get-tuple-element.9.k_ref, bf16[512,512]{1,0:T(8,128)(2,1)} %get-tuple-element.10.v_ref, bf16[2,336,512]{2,1,0:T(8,128)(2,1)} %pad_maximum_fusion.1.wo_ref), custom_call_target="tpu_custom_call" | custom-call | tf_op jit(solution)/shard_map/pallas_call | solution.py:431
  235.2 2.5 %copy.11 = bf16[512,1344]{0,1:T(8,128)(2,1)} copy(bf16[512,1344]{0,1:T(8,128)(2,1)} %bitcast.15) | data formatting | bytes 2752512
  (4 shorter events, 0.1 us)
Async XLA Ops:
  0.0 4.0 %copy-start = (bf16[336,1024]{1,0:T(8,128)(2,1)S(1)}, bf16[336,1024]{1,0:T(8,128)(2,1)}, u32[]{:S(2)}) copy-start(bf16[336,1024]{1,0:T(8,128)(2,1)} %param.10) | copy-start | bytes 2064388
  2.0 2.0 copy-start.2
  2.0 2.0 copy-start.3
  5.3 87.3 %copy-start.1 = (bf16[1024,336]{0,1:T(8,128)(2,1)S(1)}, bf16[1024,336]{0,1:T(8,128)(2,1)}, u32[]{:S(2)}) copy-start(bf16[1024,336]{0,1:T(8,128)(2,1)} %param.15) | copy-start | bytes 2064388

commit v3 on v1

v3 whole, which is shorter than its diff:
```python
import functools

import jax
import jax.numpy as jnp
from jax import lax
from jax.experimental import pallas as pl
from jax.experimental.pallas import tpu as pltpu
from jax.sharding import PartitionSpec as P

HEAD_WIDTH = 128
WINDOW = 1024
QSCALE = 168
DEPTH = 2
RING = 4
QB = 128
VMEM_BYTES = 60 * 2**20
MESH = pl.DeviceIdType.MESH
BF16 = jnp.bfloat16
F32 = jnp.float32


def place():
    seq = lax.axis_index("seq")
    return lax.rem(seq, RING), lax.axis_index("hid"), lax.div(seq, RING), lax.axis_index("rep")


def device(x, y, z, r):
    return {"seq": z * RING + x, "hid": y, "rep": r}


def step(a, by):
    return lax.rem(a + by + RING, RING)


def send(src, dst, send_sem, recv_sem, dev):
    copy = pltpu.make_async_remote_copy(
        src_ref=src,
        dst_ref=dst,
        send_sem=send_sem,
        recv_sem=recv_sem,
        device_id=dev,
        device_id_type=MESH,
    )
    copy.start()
    return copy


def greet(devs):
    barrier = pltpu.get_barrier_semaphore()
    for dev in devs:
        pl.semaphore_signal(barrier, inc=1, device_id=dev, device_id_type=MESH)
    pl.semaphore_wait(barrier, len(devs))


class Gather:
    def __init__(self, go, src, buf, c1, c2, along1, along2, sibling, sems):
        self.go, self.src, self.buf, self.c1, self.c2 = go, src, buf, c1, c2
        self.along = (along1, along2)
        self.other = sibling
        self.send, self.recv, self.ssend, self.srecv, self.loc = sems
        self.sib = []

    def piece(self, c2, c1):
        return self.buf.at[c2 * RING + c1]

    def copy(self, src, dst, i, stage, by):
        return self.go(src, dst, self.send.at[i], self.recv.at[i], self.along[stage](by))

    def to_sibling(self, ref):
        if self.other is None:
            return
        i = len(self.sib)
        self.sib.append(self.go(ref, ref, self.ssend.at[i], self.srecv.at[i], self.other))

    def start(self):
        own = self.piece(self.c2, self.c1)
        self.own = pltpu.make_async_copy(self.src, own, self.loc)
        self.own.start()
        self.a = [self.copy(self.src, own, i, 0, by) for i, by in enumerate((1, -1))]

    def pass_first(self):
        half = self.buf.shape[2] // 2
        self.b = []
        for i, by in enumerate((1, -1)):
            self.a[i].wait_recv()
            ref = self.piece(self.c2, step(self.c1, -by)).at[:, pl.ds(i * half, half)]
            self.b.append(self.copy(ref, ref, 2 + i, 0, by))

    def part(self, row, i):
        return self.buf.at[pl.ds(row * RING + 2 * i, 2)]

    def rows(self):
        self.own.wait()
        for copy in self.b:
            copy.wait_recv()
        self.early, self.late = [], []
        for group, flip in ((self.early, 0), (self.late, 1)):
            for i, by in enumerate((1, -1)):
                ref = self.part(self.c2, i ^ flip)
                group.append(self.copy(ref, ref, 4 + 2 * flip + i, 1, by))
        self.to_sibling(self.buf.at[pl.ds(self.c2 * RING, RING)])

    def pass_rows(self):
        self.f = []
        for i, by in enumerate((1, -1)):
            self.early[i].wait_recv()
            ref = self.part(step(self.c2, -by), i)
            self.f.append(self.copy(ref, ref, 8 + i, 1, by))
            self.to_sibling(ref)

    def rest(self):
        for i, by in enumerate((1, -1)):
            self.late[i].wait_recv()
            self.to_sibling(self.part(step(self.c2, -by), 1 - i))

    def last(self):
        for i in range(2):
            self.f[i].wait_recv()
            self.to_sibling(self.part(step(self.c2, 2), i))

    def done(self):
        for copy in self.sib:
            copy.wait_recv()


def block_kernel(
    tok_ref, gain_ref, wcat_ref, wo_ref, qg_ref, kg_ref, cos_ref, sin_ref,
    out_ref,
    wbuf, wobuf, xbuf, acc, sums, kvbuf, relay, heads, others, sbuf, rhalf, rfull,
    wsend, wrecv, sib_send, sib_recv, loc, tok_sem,
    ssend, srecv, xsend, xrecv, xssend, xsrecv, hsend, hrecv, osend, orecv, rsend, rrecv,
):
    x, y, z, r = place()
    width, rows = tok_ref.shape
    count = RING * RING
    seq = z * RING + x
    one = 1 - r

    def along1(by):
        return device(step(x, by * one), y, step(z, by * r), r)

    def along2(by):
        return device(step(x, by * r), y, step(z, by * one), r)

    def along_x(by):
        return device(step(x, by), y, z, r)

    def along_y(by):
        return device(x, step(y, by), z, r)

    def along_z(by):
        return device(x, y, step(z, by), r)

    def at_seq(s):
        return {"seq": s, "hid": y, "rep": r}

    def around(s):
        return lax.rem(s + count, count)

    sibling = device(x, y, z, 1 - r)
    after = at_seq(around(seq + 1))
    before = at_seq(around(seq - 1))
    onward = at_seq(around(z * RING + step(x, 1) + 2))
    origin = around(seq - 2)
    onward_from = device(step(lax.rem(origin, RING), -1), y, lax.div(origin, RING), r)
    greet([along_x(1), along_x(-1), along_z(1), along_z(-1),
           along_y(1), along_y(-1), along_y(2),
           sibling, after, before, onward, onward_from])

    sent = []

    def go(*args):
        copy = send(*args)
        sent.append(copy)
        return copy

    def sems(ph):
        return wsend.at[ph], wrecv.at[ph], sib_send, sib_recv, loc.at[ph]

    c1, c2 = x * one + z * r, z * one + x * r
    kv, qq = (Gather(go, wcat_ref.at[ph], wbuf.at[ph], c1, c2, along1, along2, None, sems(ph))
              for ph in range(2))
    oo = Gather(go, wo_ref, wobuf.at[r], c1, c2, along1, along2, sibling, sems(2))

    tok = sbuf.at[0]
    fetch = pltpu.make_async_copy(tok_ref, tok, tok_sem)
    fetch.start()
    kv.start()
    fetch.wait()

    raw = tok[...].astype(F32)
    sums[y] = jnp.sum(raw * raw, axis=0, keepdims=True)
    told = [go(sums.at[y], sums.at[y], ssend.at[i], srecv.at[i], along_y(by))
            for i, by in enumerate((1, 2, 3))]
    kv.pass_first()
    qq.start()
    for copy in told:
        copy.wait_recv()
    total = sums[0] + sums[1] + sums[2] + sums[3]
    scale = lax.rsqrt(total * (1.0 / (RING * width)) + 1e-06)

    def norm_chunk(at, size):
        part = tok[pl.ds(at, size), :].astype(F32)
        part = part * scale * gain_ref[pl.ds(at, size), :]
        xbuf[r, y, :, pl.ds(at, size)] = part.T.astype(BF16)

    lanes = 128

    def norm_step(i, carry):
        norm_chunk(pl.multiple_of(i * lanes, lanes), lanes)
        return carry

    lax.fori_loop(0, width // lanes, norm_step, 0)
    if width % lanes:
        norm_chunk(width // lanes * lanes, width % lanes)

    def x_part(block, i):
        return xbuf.at[r, block, pl.ds(i * (rows // 2), rows // 2)]

    x_sib = []

    def x_over(ref):
        i = len(x_sib)
        x_sib.append(go(ref, ref, xssend.at[i], xsrecv.at[i], sibling))

    x_early, x_late = [], []
    for group, flip in ((x_early, 0), (x_late, 1)):
        for i, by in enumerate((1, -1)):
            ref = x_part(y, i ^ flip)
            group.append(go(ref, ref, xsend.at[2 * flip + i], xrecv.at[2 * flip + i], along_y(by)))

    x_over(xbuf.at[r, y])
    kv.rows()
    qq.pass_first()
    oo.start()
    qq.rows()
    oo.pass_first()
    kv.pass_rows()
    x_last = []
    for i, by in enumerate((1, -1)):
        x_early[i].wait_recv()
        ref = x_part(step(y, -by), i)
        x_last.append(go(ref, ref, xsend.at[4 + i], xrecv.at[4 + i], along_y(by)))
        x_over(ref)
    kv.rest()
    qq.pass_rows()
    kv.last()

    def slots(kind, t, j):
        low = 1 - kind
        return t * (RING * low + kind) + j * (low + RING * kind)

    def multiply(ph, h, first):
        right = jnp.concatenate([wbuf[ph, slots(r, h, j)] for j in range(RING)], axis=0)
        for side in range(2):
            part = jnp.dot(xbuf[side, h], right, preferred_element_type=F32)
            if first:
                acc[side] = part
            else:
                acc[side] += part

    x_sib[0].wait_recv()
    multiply(0, y, True)
    for i, by in enumerate((1, -1)):
        x_late[i].wait_recv()
        x_over(x_part(step(y, -by), 1 - i))
    qq.rest()
    for copy in x_sib[1:]:
        copy.wait_recv()
    lax.fori_loop(0, 2, lambda i, c: (multiply(0, step(y, 1 + 2 * i), False), c)[1], 0)
    for i in range(2):
        x_last[i].wait_recv()
        x_over(x_part(step(y, 2), i))
    for copy in x_sib[5:]:
        copy.wait_recv()
    multiply(0, step(y, 2), False)

    cosine, sine = cos_ref[...], sin_ref[...]

    def turn(u, gain):
        u = u * lax.rsqrt(jnp.mean(u * u, axis=-1, keepdims=True) + 1e-06) * gain
        return u * cosine + pltpu.roll(u, HEAD_WIDTH // 2, 1) * sine

    def slot(i):
        return pl.ds(i * rows, rows)

    key_gain, query_gain = kg_ref[...], qg_ref[...]
    pair_width = 2 * HEAD_WIDTH

    def keys_values(side, carry):
        for head in range(2):
            cols = pl.ds(head * HEAD_WIDTH, HEAD_WIDTH)
            kvbuf[side, slot(2), cols] = turn(acc[side, :, cols], key_gain).astype(BF16)
        cols = pl.ds(pair_width, pair_width)
        kvbuf[side, slot(2), cols] = acc[side, :, cols].astype(BF16)
        return carry

    lax.fori_loop(0, 2, keys_values, 0)
    h0 = go(kvbuf.at[0, slot(2)], kvbuf.at[0, slot(1)], hsend.at[0], hrecv.at[0], after)
    h2 = go(kvbuf.at[1, slot(2)], relay, hsend.at[2], hrecv.at[2], along_x(-1))
    h1 = go(kvbuf.at[1, slot(2)], kvbuf.at[1, slot(1)], hsend.at[1], hrecv.at[1], after)

    oo.rows()
    qq.last()
    multiply(1, y, True)
    lax.fori_loop(1, RING, lambda i, c: (multiply(1, step(y, i), False), c)[1], 0)

    def queries(side, carry):
        for head in range(4):
            cols = pl.ds(head * HEAD_WIDTH, HEAD_WIDTH)
            turned = turn(acc[side, :, cols], query_gain) * QSCALE ** (-0.5)
            heads[side, :, cols] = turned.astype(BF16)
        return carry

    lax.fori_loop(0, 2, queries, 0)
    h0.wait_recv()
    h3 = go(kvbuf.at[0, slot(1)], kvbuf.at[0, slot(0)], hsend.at[3], hrecv.at[3], after)
    h2.wait_recv()
    h4 = go(relay, kvbuf.at[1, slot(0)], hsend.at[4], hrecv.at[4], onward)
    oo.pass_rows()
    oo.rest()
    for copy in (h1, h3, h4):
        copy.wait_recv()

    span = WINDOW + QB
    ri = lax.broadcasted_iota(jnp.int32, (QB, QB), 0)
    ci = lax.broadcasted_iota(jnp.int32, (QB, QB), 1)
    recent = jnp.concatenate([ci <= ri] * 2, axis=0)
    oldest = jnp.concatenate([ci > ri] * 2, axis=0)
    lane = lax.broadcasted_iota(jnp.int32, (1, span), 1)

    def attend(side, it):
        g = lax.rem(it, 2)
        i = lax.div(it, 2)
        at = pl.multiple_of(i * QB, QB)
        k_cols = pl.ds(pl.multiple_of(g * HEAD_WIDTH, HEAD_WIDTH), HEAD_WIDTH)
        v_cols = pl.ds(pl.multiple_of((2 + g) * HEAD_WIDTH, HEAD_WIDTH), HEAD_WIDTH)
        pair = [pl.ds(pl.multiple_of((2 * g + j) * HEAD_WIDTH, HEAD_WIDTH), HEAD_WIDTH)
                for j in range(2)]
        q = jnp.concatenate([heads[side, pl.ds(at, QB), c] for c in pair], axis=0)
        k = kvbuf[side, pl.ds(at, span), k_cols]
        v = kvbuf[side, pl.ds(at, span), v_cols]
        s = lax.dot_general(q, k, (((1,), (1,)), ((), ())), preferred_element_type=F32)
        present = lane + at >= DEPTH * rows - seq * rows
        s = jnp.concatenate([
            jnp.where(oldest, s[:, :QB], -jnp.inf), s[:, QB:WINDOW],
            jnp.where(recent, s[:, WINDOW:], -jnp.inf)], axis=1)
        s = jnp.where(present, s, -jnp.inf)
        p = jnp.exp(s - jnp.max(s, axis=1, keepdims=True))
        p = (p * (1.0 / jnp.sum(p, axis=1, keepdims=True))).astype(BF16)
        o = jnp.dot(p, v, preferred_element_type=F32).astype(BF16)
        for j in range(2):
            heads[side, pl.ds(at, QB), pair[j]] = o[j * QB:(j + 1) * QB]

    def attend_all(side):
        lax.fori_loop(0, 2 * (rows // QB), lambda it, c: (attend(side, it), c)[1], 0)

    attend_all(1 - r)
    swap = go(heads.at[1 - r], others, osend, orecv, sibling)
    attend_all(r)
    oo.last()
    swap.wait_recv()
    oo.done()

    depth = wobuf.shape[2]

    def terms(dest, t):
        def one_piece(j, carry):
            part = lax.dot_general(wobuf[r, slots(r, t, j)], heads[r], (((1,), (1,)), ((), ())),
                                   preferred_element_type=F32)
            part += lax.dot_general(wobuf[1 - r, slots(1 - r, t, j)], others[...],
                                    (((1,), (1,)), ((), ())), preferred_element_type=F32)
            dest[pl.ds(pl.multiple_of(j * depth, 16), depth), :] = part.astype(BF16)
            return carry

        lax.fori_loop(0, RING, one_piece, 0)

    mid = RING * depth // 2
    low, high = pl.ds(0, mid), pl.ds(mid, mid)
    terms(sbuf.at[0], step(y, 2))
    f0 = go(sbuf.at[0, low], rhalf.at[0], rsend.at[0], rrecv.at[0], along_y(1))
    f1 = go(sbuf.at[0, high], rhalf.at[1], rsend.at[1], rrecv.at[1], along_y(-1))
    terms(sbuf.at[1], step(y, 1))
    g0 = go(sbuf.at[1, high], rfull.at[0, high], rsend.at[2], rrecv.at[2], along_y(1))
    terms(sbuf.at[2], step(y, -1))
    g1 = go(sbuf.at[2, low], rfull.at[1, low], rsend.at[3], rrecv.at[3], along_y(-1))
    terms(out_ref, y)
    f0.wait_recv()
    sbuf[1, low, :] = (sbuf[1, low, :].astype(F32) + rhalf[0].astype(F32)).astype(BF16)
    g2 = go(sbuf.at[1, low], rfull.at[0, low], rsend.at[4], rrecv.at[4], along_y(1))
    f1.wait_recv()
    sbuf[2, high, :] = (sbuf[2, high, :].astype(F32) + rhalf[1].astype(F32)).astype(BF16)
    g3 = go(sbuf.at[2, high], rfull.at[1, high], rsend.at[5], rrecv.at[5], along_y(-1))
    for copy in (g0, g1, g2, g3):
        copy.wait_recv()
    out_ref[...] = (out_ref[...].astype(F32) + rfull[0].astype(F32) + rfull[1].astype(F32)).astype(BF16)
    for copy in sent:
        copy.wait_send()


def block(tok, gain, wcat, wo, query_gain, key_gain, cosine, sine):
    width, rows = tok.shape
    _, depth, cols = wcat.shape
    dma = pltpu.SemaphoreType.DMA
    vmem = pl.BlockSpec(memory_space=pltpu.VMEM)
    hbm = pl.BlockSpec(memory_space=pl.ANY)
    return pl.pallas_call(
        block_kernel,
        out_shape=jax.ShapeDtypeStruct((width, rows), BF16),
        in_specs=[hbm, vmem, hbm, hbm, vmem, vmem, vmem, vmem],
        out_specs=vmem,
        scratch_shapes=[
            pltpu.VMEM((2, RING * RING, depth, cols), BF16),
            pltpu.VMEM((2, RING * RING, depth, cols), BF16),
            pltpu.VMEM((2, RING, rows, width), BF16),
            pltpu.VMEM((2, rows, cols), F32),
            pltpu.VMEM((RING, 1, rows), F32),
            pltpu.VMEM((2, 3 * rows, cols), BF16),
            pltpu.VMEM((rows, cols), BF16),
            pltpu.VMEM((2, rows, cols), BF16),
            pltpu.VMEM((rows, cols), BF16),
            pltpu.VMEM((3, width, rows), BF16),
            pltpu.VMEM((2, width // 2, rows), BF16),
            pltpu.VMEM((2, width, rows), BF16),
            dma((3, 10)), dma((3, 10)), dma((7,)), dma((7,)), dma((3,)), dma,
            dma((3,)), dma((3,)), dma((6,)), dma((6,)), dma((7,)), dma((7,)),
            dma((5,)), dma((5,)), dma, dma, dma((6,)), dma((6,)),
        ],
        compiler_params=pltpu.CompilerParams(
            collective_id=0, has_side_effects=True, vmem_limit_bytes=VMEM_BYTES
        ),
    )(tok, gain, wcat, wo, query_gain, key_gain, cosine, sine)


def shards(tokens, norm_gain, w_query, w_key, w_value, query_gain, key_gain, w_out):
    rows, width = tokens.shape
    hid = lax.axis_index("hid")
    gain = lax.dynamic_slice_in_dim(norm_gain, hid * width, width).reshape(width, 1)
    core = lax.axis_index("rep")

    def of_core(a, axis):
        half = a.shape[axis] // 2
        return lax.dynamic_slice_in_dim(a, core * half, half, axis)

    wcat = jnp.stack([
        jnp.concatenate([of_core(w_key, 1), of_core(w_value, 1)], axis=1), of_core(w_query, 1)
    ])
    wo = of_core(w_out, 0).T
    base = lax.axis_index("seq") * rows
    qpos = base + jnp.arange(rows, dtype=jnp.int32)
    half = HEAD_WIDTH // 2
    freq = 10000.0 ** (-(jnp.arange(half, dtype=F32) * 2.0) / HEAD_WIDTH)
    angle = qpos.astype(F32)[:, None] * freq[None, :]
    cosine, sine = jnp.cos(angle), jnp.sin(angle)
    return block(
        tokens.T, gain, wcat, wo,
        query_gain.reshape(1, -1), key_gain.reshape(1, -1),
        jnp.concatenate([cosine, cosine], axis=1), jnp.concatenate([-sine, sine], axis=1),
    ).T


def solution(mesh):
    return jax.shard_map(
        shards,
        mesh=mesh,
        in_specs=(
            P(("rep", "seq"), "hid"),
            P(),
            P("seq", "hid"),
            P("seq", "hid"),
            P("seq", "hid"),
            P(),
            P(),
            P("hid", "seq"),
        ),
        out_specs=P(("rep", "seq"), "hid"),
        check_vma=False,
    )
```

time: 325 us -> 223 us (0.69)
  waiting for transfers between devices: 88.9 us -> 0 us
  Pallas kernels: 136 us -> 210 us
  matrix products: 50.3 us -> 0 us
  starting transfers between devices: 15.2 us -> 0 us
  between operations: 13.5 us -> 0.06 us
  other arithmetic: 11.7 us -> 2.95 us
    pallas_call x1, Pallas kernels: 136 us -> 210 us  [block(): pl.pallas_call(block_kernel, out_shape=jax.ShapeDtypeStruct((width, rows)...]
    reduce_scatter x1 -> x0, waiting for transfers between devices: 59.1 us -> none  [shards(): lax.psum_scatter(terms.astype(BF16), 'hid', scatter_dimension=1, tiled=True)]
    ppermute x4 -> x0, waiting for transfers between devices: 29.1 us -> none  [shifted(): return lax.ppermute(x, axis, pairs)]
    dot_general x5 -> x0, matrix products: 27.3 us -> none  [the longest x4 16.9 us: one_head(): mixed = jnp.einsum('grl,ld->rgd', probs, vpart, preferred_element_type=F32)]
    sub x4 -> x0, matrix products: 23 us -> none  [one_head(): probs = jax.nn.softmax(scores, axis=-1).astype(BF16)]
    ppermute x4 -> x0, starting transfers between devices: 15.1 us -> none  [shifted(): return lax.ppermute(x, axis, pairs)]
    and x4 -> x0, other arithmetic: 4.75 us -> none  [shards(): allowed = (diff >= 0) & (diff < WINDOW) & (kpos >= 0)[None, :]]
    transpose x2 -> x0, other arithmetic: 3.62 us -> none  [the longest x1 2.48 us: shards(): values.transpose(1, 0, 2)]
  transfers between devices with their start and end apart: 6 -> 0, of which waited for: 4 -> 0; matrix products, arithmetic and copies ran while one was open for 18% -> 0% of each run, Pallas kernels for 42% -> 0%
where the time goes in v3:
time: 223 us; the launch traced here: 219 us
  Pallas kernels  210 us (94%)
  local copies, waits for them, and re-layouts  6.45 us (3%)
  other arithmetic  2.95 us (1%)
    pallas_call x1, Pallas kernels, block(): pl.pallas_call(block_kernel, out_shape=jax.ShapeDtypeStruct((width, rows)...  210 us

profile of v3, /device:TPU:0, one launch (start us, length us, event | category | flops | bytes accessed | tf_op | source)
XLA Modules:
  0.0 219.5 jit_solution(7438480247923845303)
XLA Ops:
  0.0 0.0 copy-start
  0.0 0.9 dynamic_slice.15
  0.9 1.0 constant_dynamic-slice_fusion
  1.9 0.0 copy-start.1
  2.0 0.0 copy-done
  2.0 0.9 pad_maximum_fusion.wcat_ref
  2.9 0.2 copy-done.1
  3.1 0.8 dynamic-slice_bitcast_fusion.wo_ref
  3.9 1.1 reshape.24.gain_ref
  5.0 1.0 fusion
  6.0 1.0 pad_maximum_fusion.1
  6.9 210.0 %shard_map.82 = bf16[1344,512]{1,0:T(8,128)(2,1)} custom-call(bf16[1344,512]{1,0:T(8,128)(2,1)} %bitcast.11, f32[1344,1]{1,0:T(8,128)} %reshape.24.gain_ref, bf16[2,336,512]{2,1,0:T(8,128)(2,1)} %pad_maximum_fusion.wcat_ref, bf16[336,512]{1,0:T(8,128)(2,1)} %dynamic-slice_bitcast_fusion.wo_ref, f32[1,128]{1,0:T(1,128)} %bitcast.12, f32[1,128]{1,0:T(1,128)} %bitcast.13, ...), custom_call_target="tpu_custom_call" | custom-call | tf_op jit(solution)/shard_map/pallas_call | solution.py:407
  217.0 2.5 %copy.11 = bf16[512,1344]{0,1:T(8,128)(2,1)} copy(bf16[512,1344]{0,1:T(8,128)(2,1)} %bitcast.10) | data formatting | bytes 2752512
  (4 shorter events, 0.1 us)
Async XLA Ops:
  0.0 2.0 copy-start
  1.9 1.2 copy-start.1

commit v4 on v3

--- a/solution.py
+++ b/solution.py
@@ -126,7 +126,7 @@
 def block_kernel(
     tok_ref, gain_ref, wcat_ref, wo_ref, qg_ref, kg_ref, cos_ref, sin_ref,
     out_ref,
-    wbuf, wobuf, xbuf, acc, sums, kvbuf, relay, heads, others, sbuf, rhalf, rfull,
+    tokbuf, wbuf, wo_a, wo_b, xbuf, acc, sums, kvbuf, relay, heads, others, sbuf, rhalf, rfull,
     wsend, wrecv, sib_send, sib_recv, loc, tok_sem,
     ssend, srecv, xsend, xrecv, xssend, xsrecv, hsend, hrecv, osend, orecv, rsend, rrecv,
 ):
@@ -160,12 +160,12 @@
     sibling = device(x, y, z, 1 - r)
     after = at_seq(around(seq + 1))
     before = at_seq(around(seq - 1))
-    onward = at_seq(around(z * RING + step(x, 1) + 2))
-    origin = around(seq - 2)
-    onward_from = device(step(lax.rem(origin, RING), -1), y, lax.div(origin, RING), r)
+    via = device(step(x, -1), y, step(z, lax.div(x + 2, RING)), r)
+    back = step(x, 1)
+    via_from = device(back, y, step(z, -lax.div(back + 2, RING)), r)
     greet([along_x(1), along_x(-1), along_z(1), along_z(-1),
            along_y(1), along_y(-1), along_y(2),
-           sibling, after, before, onward, onward_from])
+           sibling, after, before, via, via_from])
 
     sent = []
 
@@ -175,14 +175,20 @@
         return copy
 
     def sems(ph):
-        return wsend.at[ph], wrecv.at[ph], sib_send, sib_recv, loc.at[ph]
+        side = max(ph - 2, 0)
+        return wsend.at[ph], wrecv.at[ph], sib_send.at[side], sib_recv.at[side], loc.at[ph]
 
     c1, c2 = x * one + z * r, z * one + x * r
     kv, qq = (Gather(go, wcat_ref.at[ph], wbuf.at[ph], c1, c2, along1, along2, None, sems(ph))
               for ph in range(2))
-    oo = Gather(go, wo_ref, wobuf.at[r], c1, c2, along1, along2, sibling, sems(2))
-
-    tok = sbuf.at[0]
+    outs = []
+    for n, buf in enumerate((wo_a, wo_b)):
+        at = pl.ds(n * wo_a.shape[2], buf.shape[2])
+        outs.append(Gather(go, wo_ref.at[at], buf.at[r], c1, c2, along1, along2, sibling,
+                           sems(2 + n)))
+    oa, ob = outs
+
+    tok = tokbuf
     fetch = pltpu.make_async_copy(tok_ref, tok, tok_sem)
     fetch.start()
     kv.start()
@@ -199,128 +205,175 @@
     total = sums[0] + sums[1] + sums[2] + sums[3]
     scale = lax.rsqrt(total * (1.0 / (RING * width)) + 1e-06)
 
-    def norm_chunk(at, size):
-        part = tok[pl.ds(at, size), :].astype(F32)
-        part = part * scale * gain_ref[pl.ds(at, size), :]
-        xbuf[r, y, :, pl.ds(at, size)] = part.T.astype(BF16)
-
     lanes = 128
-
-    def norm_step(i, carry):
-        norm_chunk(pl.multiple_of(i * lanes, lanes), lanes)
-        return carry
-
-    lax.fori_loop(0, width // lanes, norm_step, 0)
-    if width % lanes:
-        norm_chunk(width // lanes * lanes, width % lanes)
+    chunk = rows // 2
+    part_rows = chunk // 2
+
+    def rows_of(c):
+        return pl.ds(c * chunk, chunk)
+
+    def norm(c):
+        mine = scale[:, c * chunk:(c + 1) * chunk]
+
+        def norm_at(at, size):
+            part = tok[pl.ds(at, size), rows_of(c)].astype(F32)
+            part = part * mine * gain_ref[pl.ds(at, size), :]
+            xbuf[r, y, rows_of(c), pl.ds(at, size)] = part.T.astype(BF16)
+
+        def norm_step(i, carry):
+            norm_at(pl.multiple_of(i * lanes, lanes), lanes)
+            return carry
+
+        lax.fori_loop(0, width // lanes, norm_step, 0)
+        if width % lanes:
+            norm_at(width // lanes * lanes, width % lanes)
 
     def x_part(block, i):
-        return xbuf.at[r, block, pl.ds(i * (rows // 2), rows // 2)]
-
-    x_sib = []
-
-    def x_over(ref):
-        i = len(x_sib)
-        x_sib.append(go(ref, ref, xssend.at[i], xsrecv.at[i], sibling))
-
-    x_early, x_late = [], []
-    for group, flip in ((x_early, 0), (x_late, 1)):
+        return xbuf.at[r, block, pl.ds(i * part_rows, part_rows)]
+
+    x_early, x_late, x_last, x_sib = {}, {}, {}, {0: [], 1: []}
+
+    def x_over(c, ref):
+        i = 7 * c + len(x_sib[c])
+        x_sib[c].append(go(ref, ref, xssend.at[i], xsrecv.at[i], sibling))
+
+    def x_send(c):
+        for flip, group in enumerate((x_early, x_late)):
+            group[c] = []
+            for i, by in enumerate((1, -1)):
+                ref = x_part(y, 2 * c + (i ^ flip))
+                at = 6 * c + 2 * flip + i
+                group[c].append(go(ref, ref, xsend.at[at], xrecv.at[at], along_y(by)))
+        x_over(c, xbuf.at[r, y, rows_of(c)])
+
+    def x_pass(c):
+        x_last[c] = []
         for i, by in enumerate((1, -1)):
-            ref = x_part(y, i ^ flip)
-            group.append(go(ref, ref, xsend.at[2 * flip + i], xrecv.at[2 * flip + i], along_y(by)))
-
-    x_over(xbuf.at[r, y])
-    kv.rows()
-    qq.pass_first()
-    oo.start()
-    qq.rows()
-    oo.pass_first()
-    kv.pass_rows()
-    x_last = []
-    for i, by in enumerate((1, -1)):
-        x_early[i].wait_recv()
-        ref = x_part(step(y, -by), i)
-        x_last.append(go(ref, ref, xsend.at[4 + i], xrecv.at[4 + i], along_y(by)))
-        x_over(ref)
-    kv.rest()
-    qq.pass_rows()
-    kv.last()
+            x_early[c][i].wait_recv()
+            ref = x_part(step(y, -by), 2 * c + i)
+            at = 6 * c + 4 + i
+            x_last[c].append(go(ref, ref, xsend.at[at], xrecv.at[at], along_y(by)))
+            x_over(c, ref)
+
+    def x_rest(c):
+        for i, by in enumerate((1, -1)):
+            x_late[c][i].wait_recv()
+            x_over(c, x_part(step(y, -by), 2 * c + 1 - i))
+
+    def x_end(c):
+        for i in range(2):
+            x_last[c][i].wait_recv()
+            x_over(c, x_part(step(y, 2), 2 * c + i))
 
     def slots(kind, t, j):
         low = 1 - kind
         return t * (RING * low + kind) + j * (low + RING * kind)
 
-    def multiply(ph, h, first):
+    def multiply(ph, h, at, first):
         right = jnp.concatenate([wbuf[ph, slots(r, h, j)] for j in range(RING)], axis=0)
         for side in range(2):
-            part = jnp.dot(xbuf[side, h], right, preferred_element_type=F32)
+            part = jnp.dot(xbuf[side, h, at], right, preferred_element_type=F32)
             if first:
-                acc[side] = part
+                acc[side, at] = part
             else:
-                acc[side] += part
-
-    x_sib[0].wait_recv()
-    multiply(0, y, True)
-    for i, by in enumerate((1, -1)):
-        x_late[i].wait_recv()
-        x_over(x_part(step(y, -by), 1 - i))
-    qq.rest()
-    for copy in x_sib[1:]:
-        copy.wait_recv()
-    lax.fori_loop(0, 2, lambda i, c: (multiply(0, step(y, 1 + 2 * i), False), c)[1], 0)
-    for i in range(2):
-        x_last[i].wait_recv()
-        x_over(x_part(step(y, 2), i))
-    for copy in x_sib[5:]:
-        copy.wait_recv()
-    multiply(0, step(y, 2), False)
-
-    cosine, sine = cos_ref[...], sin_ref[...]
-
-    def turn(u, gain):
+                acc[side, at] += part
+
+    def turn(u, gain, at):
         u = u * lax.rsqrt(jnp.mean(u * u, axis=-1, keepdims=True) + 1e-06) * gain
-        return u * cosine + pltpu.roll(u, HEAD_WIDTH // 2, 1) * sine
-
-    def slot(i):
-        return pl.ds(i * rows, rows)
+        return u * cos_ref[at] + pltpu.roll(u, HEAD_WIDTH // 2, 1) * sin_ref[at]
 
     key_gain, query_gain = kg_ref[...], qg_ref[...]
     pair_width = 2 * HEAD_WIDTH
 
-    def keys_values(side, carry):
-        for head in range(2):
-            cols = pl.ds(head * HEAD_WIDTH, HEAD_WIDTH)
-            kvbuf[side, slot(2), cols] = turn(acc[side, :, cols], key_gain).astype(BF16)
-        cols = pl.ds(pair_width, pair_width)
-        kvbuf[side, slot(2), cols] = acc[side, :, cols].astype(BF16)
-        return carry
-
-    lax.fori_loop(0, 2, keys_values, 0)
-    h0 = go(kvbuf.at[0, slot(2)], kvbuf.at[0, slot(1)], hsend.at[0], hrecv.at[0], after)
-    h2 = go(kvbuf.at[1, slot(2)], relay, hsend.at[2], hrecv.at[2], along_x(-1))
-    h1 = go(kvbuf.at[1, slot(2)], kvbuf.at[1, slot(1)], hsend.at[1], hrecv.at[1], after)
-
-    oo.rows()
+    def block_rows(i, c):
+        return pl.ds(i * rows + c * chunk, chunk)
+
+    def keys_values(c):
+        at = rows_of(c)
+
+        def of_side(side, carry):
+            for head in range(2):
+                cols = pl.ds(head * HEAD_WIDTH, HEAD_WIDTH)
+                kvbuf[side, block_rows(2, c), cols] = turn(acc[side, at, cols], key_gain, at).astype(BF16)
+            cols = pl.ds(pair_width, pair_width)
+            kvbuf[side, block_rows(2, c), cols] = acc[side, at, cols].astype(BF16)
+            return carry
+
+        lax.fori_loop(0, 2, of_side, 0)
+
+    halo = {}
+
+    def halo_go(c, i, src, dst, dev):
+        halo[c, i] = go(src, dst, hsend.at[5 * c + i], hrecv.at[5 * c + i], dev)
+
+    def halo_send(c):
+        own0, own1 = (kvbuf.at[side, block_rows(2, c)] for side in range(2))
+        halo_go(c, 0, own0, kvbuf.at[0, block_rows(1, c)], after)
+        halo_go(c, 2, own1, relay.at[c], via)
+        halo_go(c, 1, own1, kvbuf.at[1, block_rows(1, c)], after)
+
+    def halo_pass(c):
+        halo[c, 0].wait_recv()
+        halo_go(c, 3, kvbuf.at[0, block_rows(1, c)], kvbuf.at[0, block_rows(0, c)], after)
+        halo[c, 2].wait_recv()
+        halo_go(c, 4, relay.at[c], kvbuf.at[1, block_rows(0, c)], along_x(-1))
+
+    norm(1)
+    x_send(1)
+    kv.rows()
+    qq.pass_first()
+    norm(0)
+    x_pass(1)
+    x_send(0)
+    kv.pass_rows()
+    qq.rows()
+    x_rest(1)
+    kv.rest()
+    oa.start()
+    ob.start()
+    x_end(1)
+    kv.last()
+    oa.pass_first()
+    ob.pass_first()
+    for copy in x_sib[1]:
+        copy.wait_recv()
+    multiply(0, y, rows_of(1), True)
+    lax.fori_loop(1, RING, lambda i, c: (multiply(0, step(y, i), rows_of(1), False), c)[1], 0)
+    keys_values(1)
+    halo_send(1)
+    x_pass(0)
+    qq.pass_rows()
+    x_rest(0)
+    for copy in x_sib[0]:
+        copy.wait_recv()
+    multiply(0, y, rows_of(0), True)
+    halo_pass(1)
+    lax.fori_loop(0, 2, lambda i, c: (multiply(0, step(y, 1 + 2 * i), rows_of(0), False), c)[1], 0)
+    x_end(0)
+    for copy in x_sib[0][5:]:
+        copy.wait_recv()
+    multiply(0, step(y, 2), rows_of(0), False)
+    keys_values(0)
+    halo_send(0)
+    qq.rest()
     qq.last()
-    multiply(1, y, True)
-    lax.fori_loop(1, RING, lambda i, c: (multiply(1, step(y, i), False), c)[1], 0)
+    whole = pl.ds(0, rows)
+    multiply(1, y, whole, True)
+    lax.fori_loop(1, RING, lambda i, c: (multiply(1, step(y, i), whole, False), c)[1], 0)
 
     def queries(side, carry):
         for head in range(4):
             cols = pl.ds(head * HEAD_WIDTH, HEAD_WIDTH)
-            turned = turn(acc[side, :, cols], query_gain) * QSCALE ** (-0.5)
+            turned = turn(acc[side, :, cols], query_gain, whole) * QSCALE ** (-0.5)
             heads[side, :, cols] = turned.astype(BF16)
         return carry
 
     lax.fori_loop(0, 2, queries, 0)
-    h0.wait_recv()
-    h3 = go(kvbuf.at[0, slot(1)], kvbuf.at[0, slot(0)], hsend.at[3], hrecv.at[3], after)
-    h2.wait_recv()
-    h4 = go(relay, kvbuf.at[1, slot(0)], hsend.at[4], hrecv.at[4], onward)
-    oo.pass_rows()
-    oo.rest()
-    for copy in (h1, h3, h4):
-        copy.wait_recv()
+    halo_pass(0)
+    oa.rows()
+    for c in (1, 0):
+        for i in (1, 3, 4):
+            halo[c, i].wait_recv()
 
     span = WINDOW + QB
     ri = lax.broadcasted_iota(jnp.int32, (QB, QB), 0)
@@ -357,43 +410,75 @@
 
     attend_all(1 - r)
     swap = go(heads.at[1 - r], others, osend, orecv, sibling)
+    oa.pass_rows()
+    ob.rows()
     attend_all(r)
-    oo.last()
+    oa.rest()
+    oa.last()
     swap.wait_recv()
-    oo.done()
-
-    depth = wobuf.shape[2]
-
-    def terms(dest, t):
+
+    depth = wo_a.shape[2] + wo_b.shape[2]
+    near, far = pl.ds(0, chunk), pl.ds(chunk, chunk)
+    flows = {}
+
+    def terms(n, t, dest):
+        buf = (wo_a, wo_b)[n]
+        start, size = n * wo_a.shape[2], buf.shape[2]
+
         def one_piece(j, carry):
-            part = lax.dot_general(wobuf[r, slots(r, t, j)], heads[r], (((1,), (1,)), ((), ())),
+            part = lax.dot_general(buf[r, slots(r, t, j)], heads[r], (((1,), (1,)), ((), ())),
                                    preferred_element_type=F32)
-            part += lax.dot_general(wobuf[1 - r, slots(1 - r, t, j)], others[...],
+            part += lax.dot_general(buf[1 - r, slots(1 - r, t, j)], others[...],
                                     (((1,), (1,)), ((), ())), preferred_element_type=F32)
-            dest[pl.ds(pl.multiple_of(j * depth, 16), depth), :] = part.astype(BF16)
+            dest[j, pl.ds(start, size), :] = part.astype(BF16)
             return carry
 
         lax.fori_loop(0, RING, one_piece, 0)
 
-    mid = RING * depth // 2
-    low, high = pl.ds(0, mid), pl.ds(mid, mid)
-    terms(sbuf.at[0], step(y, 2))
-    f0 = go(sbuf.at[0, low], rhalf.at[0], rsend.at[0], rrecv.at[0], along_y(1))
-    f1 = go(sbuf.at[0, high], rhalf.at[1], rsend.at[1], rrecv.at[1], along_y(-1))
-    terms(sbuf.at[1], step(y, 1))
-    g0 = go(sbuf.at[1, high], rfull.at[0, high], rsend.at[2], rrecv.at[2], along_y(1))
-    terms(sbuf.at[2], step(y, -1))
-    g1 = go(sbuf.at[2, low], rfull.at[1, low], rsend.at[3], rrecv.at[3], along_y(-1))
-    terms(out_ref, y)
-    f0.wait_recv()
-    sbuf[1, low, :] = (sbuf[1, low, :].astype(F32) + rhalf[0].astype(F32)).astype(BF16)
-    g2 = go(sbuf.at[1, low], rfull.at[0, low], rsend.at[4], rrecv.at[4], along_y(1))
-    f1.wait_recv()
-    sbuf[2, high, :] = (sbuf[2, high, :].astype(F32) + rhalf[1].astype(F32)).astype(BF16)
-    g3 = go(sbuf.at[2, high], rfull.at[1, high], rsend.at[5], rrecv.at[5], along_y(-1))
-    for copy in (g0, g1, g2, g3):
-        copy.wait_recv()
-    out_ref[...] = (out_ref[...].astype(F32) + rfull[0].astype(F32) + rfull[1].astype(F32)).astype(BF16)
+    def cut(n):
+        return pl.ds(n * wo_a.shape[2], (wo_a, wo_b)[n].shape[2])
+
+    def flow(n, i, src, dst, by):
+        flows[n, i] = go(src, dst, rsend.at[6 * n + i], rrecv.at[6 * n + i], along_y(by))
+
+    def spread(n):
+        at = cut(n)
+        terms(n, step(y, 2), sbuf.at[0])
+        flow(n, 0, sbuf.at[0, :, at, near], rhalf.at[0, :, at], 1)
+        flow(n, 1, sbuf.at[0, :, at, far], rhalf.at[1, :, at], -1)
+        terms(n, step(y, 1), sbuf.at[1])
+        flow(n, 2, sbuf.at[1, :, at, far], rfull.at[0, :, at, far], 1)
+        terms(n, step(y, -1), sbuf.at[2])
+        flow(n, 3, sbuf.at[2, :, at, near], rfull.at[1, :, at, near], -1)
+
+    def add(n):
+        at = cut(n)
+        for i, half, by in ((0, near, 1), (1, far, -1)):
+            flows[n, i].wait_recv()
+            both = sbuf[1 + i, :, at, half].astype(F32) + rhalf[i, :, at].astype(F32)
+            sbuf[1 + i, :, at, half] = both.astype(BF16)
+            flow(n, 4 + i, sbuf.at[1 + i, :, at, half], rfull.at[i, :, at, half], by)
+
+    def close(n):
+        at = cut(n)
+        for i in range(2, 6):
+            flows[n, i].wait_recv()
+        out_ref[:, at, :] = (out_ref[:, at, :].astype(F32) + rfull[0, :, at, :].astype(F32)
+                             + rfull[1, :, at, :].astype(F32)).astype(BF16)
+
+    oa.done()
+    spread(0)
+    ob.pass_rows()
+    terms(0, y, out_ref)
+    add(0)
+    ob.rest()
+    ob.last()
+    ob.done()
+    spread(1)
+    terms(1, y, out_ref)
+    add(1)
+    close(0)
+    close(1)
     for copy in sent:
         copy.wait_send()
 
@@ -401,30 +486,33 @@
 def block(tok, gain, wcat, wo, query_gain, key_gain, cosine, sine):
     width, rows = tok.shape
     _, depth, cols = wcat.shape
+    first = -(-depth // 32) * 16
     dma = pltpu.SemaphoreType.DMA
     vmem = pl.BlockSpec(memory_space=pltpu.VMEM)
     hbm = pl.BlockSpec(memory_space=pl.ANY)
     return pl.pallas_call(
         block_kernel,
-        out_shape=jax.ShapeDtypeStruct((width, rows), BF16),
+        out_shape=jax.ShapeDtypeStruct((RING, depth, rows), BF16),
         in_specs=[hbm, vmem, hbm, hbm, vmem, vmem, vmem, vmem],
         out_specs=vmem,
         scratch_shapes=[
+            pltpu.VMEM((width, rows), BF16),
             pltpu.VMEM((2, RING * RING, depth, cols), BF16),
-            pltpu.VMEM((2, RING * RING, depth, cols), BF16),
+            pltpu.VMEM((2, RING * RING, first, cols), BF16),
+            pltpu.VMEM((2, RING * RING, depth - first, cols), BF16),
             pltpu.VMEM((2, RING, rows, width), BF16),
             pltpu.VMEM((2, rows, cols), F32),
             pltpu.VMEM((RING, 1, rows), F32),
             pltpu.VMEM((2, 3 * rows, cols), BF16),
-            pltpu.VMEM((rows, cols), BF16),
+            pltpu.VMEM((2, rows // 2, cols), BF16),
             pltpu.VMEM((2, rows, cols), BF16),
             pltpu.VMEM((rows, cols), BF16),
-            pltpu.VMEM((3, width, rows), BF16),
-            pltpu.VMEM((2, width // 2, rows), BF16),
-            pltpu.VMEM((2, width, rows), BF16),
-            dma((3, 10)), dma((3, 10)), dma((7,)), dma((7,)), dma((3,)), dma,
-            dma((3,)), dma((3,)), dma((6,)), dma((6,)), dma((7,)), dma((7,)),
-            dma((5,)), dma((5,)), dma, dma, dma((6,)), dma((6,)),
+            pltpu.VMEM((3, RING, depth, rows), BF16),
+            pltpu.VMEM((2, RING, depth, rows // 2), BF16),
+            pltpu.VMEM((2, RING, depth, rows), BF16),
+            dma((4, 10)), dma((4, 10)), dma((2, 7)), dma((2, 7)), dma((4,)), dma,
+            dma((3,)), dma((3,)), dma((12,)), dma((12,)), dma((14,)), dma((14,)),
+            dma((10,)), dma((10,)), dma, dma, dma((12,)), dma((12,)),
         ],
         compiler_params=pltpu.CompilerParams(
             collective_id=0, has_side_effects=True, vmem_limit_bytes=VMEM_BYTES
@@ -456,7 +544,7 @@
         tokens.T, gain, wcat, wo,
         query_gain.reshape(1, -1), key_gain.reshape(1, -1),
         jnp.concatenate([cosine, cosine], axis=1), jnp.concatenate([-sine, sine], axis=1),
-    ).T
+    ).reshape(width, rows).T
 
 
 def solution(mesh):

time: 223 us -> 186 us (0.83); the launches traced: 219 us -> 186 us
  Pallas kernels: 210 us -> 176 us
    pallas_call x1, Pallas kernels: 210 us -> 176 us  [block(): pl.pallas_call(block_kernel, out_shape=jax.ShapeDtypeStruct((RING, depth,...]
where the time goes in v4:
time: 186 us
  Pallas kernels  176 us (95%)
  local copies, waits for them, and re-layouts  6.45 us (3%)
  other arithmetic  2.95 us (2%)
    pallas_call x1, Pallas kernels, block(): pl.pallas_call(block_kernel, out_shape=jax.ShapeDtypeStruct((RING, depth,...  176 us

profile of v4, /device:TPU:0, one launch (start us, length us, event | category | flops | bytes accessed | tf_op | source)
XLA Modules:
  0.0 185.7 jit_solution(12959364235582820372)
XLA Ops:
  0.0 0.0 copy-start
  0.0 0.9 dynamic_slice.15
  0.9 1.0 constant_dynamic-slice_fusion
  1.9 0.0 copy-start.1
  2.0 0.0 copy-done
  2.0 0.9 pad_maximum_fusion.wcat_ref
  2.9 0.2 copy-done.1
  3.1 0.8 dynamic-slice_bitcast_fusion.wo_ref
  3.9 1.1 reshape.28.gain_ref
  5.0 1.0 fusion
  6.0 1.0 pad_maximum_fusion.1
  6.9 176.2 %shard_map.82 = bf16[4,336,512]{2,1,0:T(8,128)(2,1)} custom-call(bf16[1344,512]{1,0:T(8,128)(2,1)} %bitcast.13, f32[1344,1]{1,0:T(8,128)} %reshape.28.gain_ref, bf16[2,336,512]{2,1,0:T(8,128)(2,1)} %pad_maximum_fusion.wcat_ref, bf16[336,512]{1,0:T(8,128)(2,1)} %dynamic-slice_bitcast_fusion.wo_ref, f32[1,128]{1,0:T(1,128)} %bitcast.14, f32[1,128]{1,0:T(1,128)} %bitcast.15, ...), custom_call_target="tpu_custom_call" | custom-call | tf_op jit(solution)/shard_map/pallas_call | solution.py:493
  183.2 2.5 %copy.11 = bf16[512,1344]{0,1:T(8,128)(2,1)} copy(bf16[512,1344]{0,1:T(8,128)(2,1)} %bitcast.12) | data formatting | bytes 2752512
  (4 shorter events, 0.1 us)
Async XLA Ops:
  0.0 2.0 %copy-start = (bf16[336,1024]{1,0:T(8,128)(2,1)S(1)}, bf16[336,1024]{1,0:T(8,128)(2,1)}, u32[]{:S(2)}) copy-start(bf16[336,1024]{1,0:T(8,128)(2,1)} %param.10) | copy-start | bytes 2064388
  1.9 1.2 copy-start.1

commit v5 on v4

--- a/solution.py
+++ b/solution.py
@@ -13,6 +13,7 @@
 DEPTH = 2
 RING = 4
 QB = 128
+OUT_PARTS = (176, 160)
 VMEM_BYTES = 60 * 2**20
 MESH = pl.DeviceIdType.MESH
 BF16 = jnp.bfloat16
@@ -49,16 +50,21 @@
     barrier = pltpu.get_barrier_semaphore()
     for dev in devs:
         pl.semaphore_signal(barrier, inc=1, device_id=dev, device_id_type=MESH)
-    pl.semaphore_wait(barrier, len(devs))
+    return lambda: pl.semaphore_wait(barrier, len(devs))
 
 
 class Gather:
     def __init__(self, go, src, buf, c1, c2, along1, along2, sibling, sems):
-        self.go, self.src, self.buf, self.c1, self.c2 = go, src, buf, c1, c2
+        self.go, self.buf, self.c1, self.c2 = go, buf, c1, c2
         self.along = (along1, along2)
         self.other = sibling
         self.send, self.recv, self.ssend, self.srecv, self.loc = sems
         self.sib = []
+        self.own = []
+        for i, (part, at, size) in enumerate(src):
+            to = self.piece(c2, c1).at[:, pl.ds(at, size)]
+            self.own.append(pltpu.make_async_copy(part, to, self.loc.at[i]))
+            self.own[i].start()
 
     def piece(self, c2, c1):
         return self.buf.at[c2 * RING + c1]
@@ -74,9 +80,9 @@
 
     def start(self):
         own = self.piece(self.c2, self.c1)
-        self.own = pltpu.make_async_copy(self.src, own, self.loc)
-        self.own.start()
-        self.a = [self.copy(self.src, own, i, 0, by) for i, by in enumerate((1, -1))]
+        for copy in self.own:
+            copy.wait()
+        self.a = [self.copy(own, own, i, 0, by) for i, by in enumerate((1, -1))]
 
     def pass_first(self):
         half = self.buf.shape[2] // 2
@@ -90,7 +96,6 @@
         return self.buf.at[pl.ds(row * RING + 2 * i, 2)]
 
     def rows(self):
-        self.own.wait()
         for copy in self.b:
             copy.wait_recv()
         self.early, self.late = [], []
@@ -124,9 +129,9 @@
 
 
 def block_kernel(
-    tok_ref, gain_ref, wcat_ref, wo_ref, qg_ref, kg_ref, cos_ref, sin_ref,
+    tok_ref, gain_ref, wq_ref, wk_ref, wv_ref, wo_ref, qg_ref, kg_ref, cos_ref, sin_ref,
     out_ref,
-    tokbuf, wbuf, wo_a, wo_b, xbuf, acc, sums, kvbuf, relay, heads, others, sbuf, rhalf, rfull,
+    tokbuf, wbuf, wo_bufs, xbuf, acc, sums, kvbuf, relay, heads, others, sbuf, rhalf, rfull,
     wsend, wrecv, sib_send, sib_recv, loc, tok_sem,
     ssend, srecv, xsend, xrecv, xssend, xsrecv, hsend, hrecv, osend, orecv, rsend, rrecv,
 ):
@@ -163,9 +168,9 @@
     via = device(step(x, -1), y, step(z, lax.div(x + 2, RING)), r)
     back = step(x, 1)
     via_from = device(back, y, step(z, -lax.div(back + 2, RING)), r)
-    greet([along_x(1), along_x(-1), along_z(1), along_z(-1),
-           along_y(1), along_y(-1), along_y(2),
-           sibling, after, before, via, via_from])
+    arrived = greet([along_x(1), along_x(-1), along_z(1), along_z(-1),
+                     along_y(1), along_y(-1), along_y(2),
+                     sibling, after, before, via, via_from])
 
     sent = []
 
@@ -179,27 +184,37 @@
         return wsend.at[ph], wrecv.at[ph], sib_send.at[side], sib_recv.at[side], loc.at[ph]
 
     c1, c2 = x * one + z * r, z * one + x * r
-    kv, qq = (Gather(go, wcat_ref.at[ph], wbuf.at[ph], c1, c2, along1, along2, None, sems(ph))
-              for ph in range(2))
-    outs = []
-    for n, buf in enumerate((wo_a, wo_b)):
-        at = pl.ds(n * wo_a.shape[2], buf.shape[2])
-        outs.append(Gather(go, wo_ref.at[at], buf.at[r], c1, c2, along1, along2, sibling,
-                           sems(2 + n)))
-    oa, ob = outs
+    cols, depth = wbuf.shape[3], wbuf.shape[2]
+    half = cols // 2
+
+    def core_cols(size):
+        return pl.ds(pl.multiple_of(r * size, size), size)
 
     tok = tokbuf
     fetch = pltpu.make_async_copy(tok_ref, tok, tok_sem)
+    kv = Gather(go, [(wk_ref.at[:, core_cols(half)], 0, half), (wv_ref.at[:, core_cols(half)], half, half)],
+                wbuf.at[0], c1, c2, along1, along2, None, sems(0))
     fetch.start()
-    kv.start()
+    qq = Gather(go, [(wq_ref.at[:, core_cols(cols)], 0, cols)],
+                wbuf.at[1], c1, c2, along1, along2, None, sems(1))
+    outs, starts = [], []
+    for n, buf in enumerate(wo_bufs):
+        starts.append(sum(b.shape[2] for b in wo_bufs[:n]))
+        src = wo_ref.at[pl.ds(starts[n], buf.shape[2]), core_cols(cols)]
+        outs.append(Gather(go, [(src, 0, cols)], buf.at[r], c1, c2, along1, along2, sibling,
+                           sems(2 + n)))
+
     fetch.wait()
-
     raw = tok[...].astype(F32)
     sums[y] = jnp.sum(raw * raw, axis=0, keepdims=True)
+    arrived()
+    kv.start()
     told = [go(sums.at[y], sums.at[y], ssend.at[i], srecv.at[i], along_y(by))
             for i, by in enumerate((1, 2, 3))]
-    kv.pass_first()
-    qq.start()
+    for one_of in (qq, *outs):
+        one_of.start()
+    for one_of in (kv, qq, *outs):
+        one_of.pass_first()
     for copy in told:
         copy.wait_recv()
     total = sums[0] + sums[1] + sums[2] + sums[3]
@@ -209,6 +224,8 @@
     chunk = rows // 2
     part_rows = chunk // 2
 
+    skew = lax.rem(y * width, lanes)
+
     def rows_of(c):
         return pl.ds(c * chunk, chunk)
 
@@ -217,8 +234,10 @@
 
         def norm_at(at, size):
             part = tok[pl.ds(at, size), rows_of(c)].astype(F32)
-            part = part * mine * gain_ref[pl.ds(at, size), :]
-            xbuf[r, y, rows_of(c), pl.ds(at, size)] = part.T.astype(BF16)
+            wide = 2 * size if size == lanes else lanes
+            seen = gain_ref[:, pl.ds(pl.multiple_of(y * width - skew + at, lanes), wide)]
+            gain = jnp.where(skew == 0, seen[:, :size], seen[:, lanes // 2:lanes // 2 + size])
+            xbuf[r, y, rows_of(c), pl.ds(at, size)] = ((part * mine).T * gain).astype(BF16)
 
         def norm_step(i, carry):
             norm_at(pl.multiple_of(i * lanes, lanes), lanes)
@@ -280,7 +299,10 @@
 
     def turn(u, gain, at):
         u = u * lax.rsqrt(jnp.mean(u * u, axis=-1, keepdims=True) + 1e-06) * gain
-        return u * cos_ref[at] + pltpu.roll(u, HEAD_WIDTH // 2, 1) * sin_ref[at]
+        cosine, sine = cos_ref[at], sin_ref[at]
+        cosine = jnp.concatenate([cosine, cosine], axis=1)
+        sine = jnp.concatenate([-sine, sine], axis=1)
+        return u * cosine + pltpu.roll(u, HEAD_WIDTH // 2, 1) * sine
 
     key_gain, query_gain = kg_ref[...], qg_ref[...]
     pair_width = 2 * HEAD_WIDTH
@@ -321,7 +343,6 @@
     norm(1)
     x_send(1)
     kv.rows()
-    qq.pass_first()
     norm(0)
     x_pass(1)
     x_send(0)
@@ -329,12 +350,8 @@
     qq.rows()
     x_rest(1)
     kv.rest()
-    oa.start()
-    ob.start()
     x_end(1)
     kv.last()
-    oa.pass_first()
-    ob.pass_first()
     for copy in x_sib[1]:
         copy.wait_recv()
     multiply(0, y, rows_of(1), True)
@@ -370,7 +387,7 @@
 
     lax.fori_loop(0, 2, queries, 0)
     halo_pass(0)
-    oa.rows()
+    outs[0].rows()
     for c in (1, 0):
         for i in (1, 3, 4):
             halo[c, i].wait_recv()
@@ -410,20 +427,19 @@
 
     attend_all(1 - r)
     swap = go(heads.at[1 - r], others, osend, orecv, sibling)
-    oa.pass_rows()
-    ob.rows()
+    outs[0].pass_rows()
+    outs[1].rows()
     attend_all(r)
-    oa.rest()
-    oa.last()
+    outs[0].rest()
+    outs[0].last()
     swap.wait_recv()
 
-    depth = wo_a.shape[2] + wo_b.shape[2]
     near, far = pl.ds(0, chunk), pl.ds(chunk, chunk)
     flows = {}
 
     def terms(n, t, dest):
-        buf = (wo_a, wo_b)[n]
-        start, size = n * wo_a.shape[2], buf.shape[2]
+        buf = wo_bufs[n]
+        start, size = starts[n], buf.shape[2]
 
         def one_piece(j, carry):
             part = lax.dot_general(buf[r, slots(r, t, j)], heads[r], (((1,), (1,)), ((), ())),
@@ -436,7 +452,7 @@
         lax.fori_loop(0, RING, one_piece, 0)
 
     def cut(n):
-        return pl.ds(n * wo_a.shape[2], (wo_a, wo_b)[n].shape[2])
+        return pl.ds(starts[n], wo_bufs[n].shape[2])
 
     def flow(n, i, src, dst, by):
         flows[n, i] = go(src, dst, rsend.at[6 * n + i], rrecv.at[6 * n + i], along_y(by))
@@ -466,40 +482,40 @@
         out_ref[:, at, :] = (out_ref[:, at, :].astype(F32) + rfull[0, :, at, :].astype(F32)
                              + rfull[1, :, at, :].astype(F32)).astype(BF16)
 
-    oa.done()
-    spread(0)
-    ob.pass_rows()
-    terms(0, y, out_ref)
-    add(0)
-    ob.rest()
-    ob.last()
-    ob.done()
-    spread(1)
-    terms(1, y, out_ref)
-    add(1)
-    close(0)
-    close(1)
+    for n in range(len(outs)):
+        outs[n].done()
+        spread(n)
+        if n + 1 < len(outs):
+            outs[n + 1].pass_rows()
+        if n + 2 < len(outs):
+            outs[n + 2].rows()
+        terms(n, y, out_ref)
+        add(n)
+        if n + 1 < len(outs):
+            outs[n + 1].rest()
+            outs[n + 1].last()
+    for n in range(len(outs)):
+        close(n)
     for copy in sent:
         copy.wait_send()
 
 
-def block(tok, gain, wcat, wo, query_gain, key_gain, cosine, sine):
+def block(tok, gain, wq, wk, wv, wo, query_gain, key_gain, cosine, sine):
     width, rows = tok.shape
-    _, depth, cols = wcat.shape
-    first = -(-depth // 32) * 16
+    depth, cols = wk.shape
+    parts = len(OUT_PARTS)
     dma = pltpu.SemaphoreType.DMA
     vmem = pl.BlockSpec(memory_space=pltpu.VMEM)
     hbm = pl.BlockSpec(memory_space=pl.ANY)
     return pl.pallas_call(
         block_kernel,
         out_shape=jax.ShapeDtypeStruct((RING, depth, rows), BF16),
-        in_specs=[hbm, vmem, hbm, hbm, vmem, vmem, vmem, vmem],
+        in_specs=[hbm, vmem, hbm, hbm, hbm, hbm, vmem, vmem, vmem, vmem],
         out_specs=vmem,
         scratch_shapes=[
             pltpu.VMEM((width, rows), BF16),
             pltpu.VMEM((2, RING * RING, depth, cols), BF16),
-            pltpu.VMEM((2, RING * RING, first, cols), BF16),
-            pltpu.VMEM((2, RING * RING, depth - first, cols), BF16),
+            [pltpu.VMEM((2, RING * RING, size, cols), BF16) for size in OUT_PARTS],
             pltpu.VMEM((2, RING, rows, width), BF16),
             pltpu.VMEM((2, rows, cols), F32),
             pltpu.VMEM((RING, 1, rows), F32),
@@ -510,30 +526,19 @@
             pltpu.VMEM((3, RING, depth, rows), BF16),
             pltpu.VMEM((2, RING, depth, rows // 2), BF16),
             pltpu.VMEM((2, RING, depth, rows), BF16),
-            dma((4, 10)), dma((4, 10)), dma((2, 7)), dma((2, 7)), dma((4,)), dma,
+            dma((2 + parts, 10)), dma((2 + parts, 10)), dma((parts, 7)), dma((parts, 7)),
+            dma((2 + parts, 2)), dma,
             dma((3,)), dma((3,)), dma((12,)), dma((12,)), dma((14,)), dma((14,)),
-            dma((10,)), dma((10,)), dma, dma, dma((12,)), dma((12,)),
+            dma((10,)), dma((10,)), dma, dma, dma((6 * parts,)), dma((6 * parts,)),
         ],
         compiler_params=pltpu.CompilerParams(
             collective_id=0, has_side_effects=True, vmem_limit_bytes=VMEM_BYTES
         ),
-    )(tok, gain, wcat, wo, query_gain, key_gain, cosine, sine)
+    )(tok, gain, wq, wk, wv, wo, query_gain, key_gain, cosine, sine)
 
 
 def shards(tokens, norm_gain, w_query, w_key, w_value, query_gain, key_gain, w_out):
     rows, width = tokens.shape
-    hid = lax.axis_index("hid")
-    gain = lax.dynamic_slice_in_dim(norm_gain, hid * width, width).reshape(width, 1)
-    core = lax.axis_index("rep")
-
-    def of_core(a, axis):
-        half = a.shape[axis] // 2
-        return lax.dynamic_slice_in_dim(a, core * half, half, axis)
-
-    wcat = jnp.stack([
-        jnp.concatenate([of_core(w_key, 1), of_core(w_value, 1)], axis=1), of_core(w_query, 1)
-    ])
-    wo = of_core(w_out, 0).T
     base = lax.axis_index("seq") * rows
     qpos = base + jnp.arange(rows, dtype=jnp.int32)
     half = HEAD_WIDTH // 2
@@ -541,9 +546,8 @@
     angle = qpos.astype(F32)[:, None] * freq[None, :]
     cosine, sine = jnp.cos(angle), jnp.sin(angle)
     return block(
-        tokens.T, gain, wcat, wo,
-        query_gain.reshape(1, -1), key_gain.reshape(1, -1),
-        jnp.concatenate([cosine, cosine], axis=1), jnp.concatenate([-sine, sine], axis=1),
+        tokens.T, norm_gain.reshape(1, -1), w_query, w_key, w_value, w_out.T,
+        query_gain.reshape(1, -1), key_gain.reshape(1, -1), cosine, sine,
     ).reshape(width, rows).T
 
 

time: 186 us -> 180 us (0.968)
  local copies, waits for them, and re-layouts: 6.45 us -> 3.87 us
  Pallas kernels: 176 us -> 174 us
    pallas_call x1, Pallas kernels: 176 us -> 174 us  [block(): pl.pallas_call(block_kernel, out_shape=jax.ShapeDtypeStruct((RING, depth,...]
    dynamic_slice x2 -> x0, local copies, waits for them, and re-layouts: 1.88 us -> none  [the longest x1 1.03 us: of_core(): return lax.dynamic_slice_in_dim(a, core * half, half, axis)]
where the time goes in v5:
time: 180 us
  Pallas kernels  174 us (97%)
  local copies, waits for them, and re-layouts  3.87 us (2%)
    pallas_call x1, Pallas kernels, block(): pl.pallas_call(block_kernel, out_shape=jax.ShapeDtypeStruct((RING, depth,...  174 us

profile of v5, /device:TPU:0, one launch (start us, length us, event | category | flops | bytes accessed | tf_op | source)
XLA Modules:
  0.0 179.7 jit_solution(152056977230518184)
XLA Ops:
  0.0 1.4 reshape.24.gain_ref
  1.4 1.8 multiply_sine_fusion
  3.2 174.0 %shard_map.82 = bf16[4,336,512]{2,1,0:T(8,128)(2,1)} custom-call(bf16[1344,512]{1,0:T(8,128)(2,1)} %bitcast.8, f32[1,5376]{1,0:T(1,128)} %reshape.24.gain_ref, bf16[336,1024]{1,0:T(8,128)(2,1)} %wq_ref.1, bf16[336,512]{1,0:T(8,128)(2,1)} %wk_ref.1, bf16[336,512]{1,0:T(8,128)(2,1)} %wv_ref.1, bf16[336,1024]{1,0:T(8,128)(2,1)} %bitcast.9, f32[1,128]{1,0:T(1,128)} %bitcast.10, ...), custom_call_target="tpu_custom_call" | custom-call | tf_op jit(solution)/shard_map/pallas_call | solution.py:510
  177.2 2.5 %copy.10 = bf16[512,1344]{0,1:T(8,128)(2,1)} copy(bf16[512,1344]{0,1:T(8,128)(2,1)} %bitcast.7) | data formatting | bytes 2752512
  (2 shorter events, 0.0 us)

commit v6 on v5

--- a/solution.py
+++ b/solution.py
@@ -13,7 +13,7 @@
 DEPTH = 2
 RING = 4
 QB = 128
-OUT_PARTS = (176, 160)
+OUT_PARTS = (144, 192)
 VMEM_BYTES = 60 * 2**20
 MESH = pl.DeviceIdType.MESH
 BF16 = jnp.bfloat16
@@ -60,6 +60,7 @@
         self.other = sibling
         self.send, self.recv, self.ssend, self.srecv, self.loc = sems
         self.sib = []
+        self.low = 2
         self.own = []
         for i, (part, at, size) in enumerate(src):
             to = self.piece(c2, c1).at[:, pl.ds(at, size)]
@@ -93,7 +94,7 @@
             self.b.append(self.copy(ref, ref, 2 + i, 0, by))
 
     def part(self, row, i):
-        return self.buf.at[pl.ds(row * RING + 2 * i, 2)]
+        return self.buf.at[pl.ds(row * RING + self.low * i, RING - self.low if i else self.low)]
 
     def rows(self):
         for copy in self.b:
@@ -197,6 +198,7 @@
     fetch.start()
     qq = Gather(go, [(wq_ref.at[:, core_cols(cols)], 0, cols)],
                 wbuf.at[1], c1, c2, along1, along2, None, sems(1))
+    qq.low = 1
     outs, starts = [], []
     for n, buf in enumerate(wo_bufs):
         starts.append(sum(b.shape[2] for b in wo_bufs[:n]))

time: 180 us -> 178 us (0.989)
  Pallas kernels: 174 us -> 172 us
    pallas_call x1, Pallas kernels: 174 us -> 172 us  [block(): pl.pallas_call(block_kernel, out_shape=jax.ShapeDtypeStruct((RING, depth,...]
where the time goes in v6:
time: 178 us
  Pallas kernels  172 us (97%)
  local copies, waits for them, and re-layouts  3.87 us (2%)
  other arithmetic  1.79 us (1%)
    pallas_call x1, Pallas kernels, block(): pl.pallas_call(block_kernel, out_shape=jax.ShapeDtypeStruct((RING, depth,...  172 us

profile of v6, /device:TPU:0, one launch (start us, length us, event | category | flops | bytes accessed | tf_op | source)
XLA Modules:
  0.0 177.6 jit_solution(15820592274472727705)
XLA Ops:
  0.0 1.4 reshape.24.gain_ref
  1.4 1.8 %multiply_sine_fusion = (f32[512,64]{1,0:T(8,128)}, f32[512,64]{1,0:T(8,128)}) fusion(f32[64]{0:T(128)S(1)} %multiply_power_fusion, f32[512]{0:T(512)S(1)} %add_convert_fusion), kind=kLoop, calls=%fused_computation | loop fusion | flops 32768 | bytes 264448 | tf_op jit(solution)/shard_map/sin | solution.py:549
  3.2 171.9 %shard_map.82 = bf16[4,336,512]{2,1,0:T(8,128)(2,1)} custom-call(bf16[1344,512]{1,0:T(8,128)(2,1)} %bitcast.8, f32[1,5376]{1,0:T(1,128)} %reshape.24.gain_ref, bf16[336,1024]{1,0:T(8,128)(2,1)} %wq_ref.1, bf16[336,512]{1,0:T(8,128)(2,1)} %wk_ref.1, bf16[336,512]{1,0:T(8,128)(2,1)} %wv_ref.1, bf16[336,1024]{1,0:T(8,128)(2,1)} %bitcast.9, f32[1,128]{1,0:T(1,128)} %bitcast.10, ...), custom_call_target="tpu_custom_call" | custom-call | tf_op jit(solution)/shard_map/pallas_call | solution.py:512
  175.1 2.5 %copy.10 = bf16[512,1344]{0,1:T(8,128)(2,1)} copy(bf16[512,1344]{0,1:T(8,128)(2,1)} %bitcast.7) | data formatting | bytes 2752512
  (2 shorter events, 0.0 us)

commit v7 on v6

--- a/solution.py
+++ b/solution.py
@@ -346,10 +346,10 @@
     x_send(1)
     kv.rows()
     norm(0)
+    kv.pass_rows()
+    qq.rows()
     x_pass(1)
     x_send(0)
-    kv.pass_rows()
-    qq.rows()
     x_rest(1)
     kv.rest()
     x_end(1)

time: 178 us -> 178 us (level)
  no operation moved by 1% of the time
where the time goes in v7:
time: 178 us
  Pallas kernels  172 us (97%)
  local copies, waits for them, and re-layouts  3.87 us (2%)
  other arithmetic  1.79 us (1%)
    pallas_call x1, Pallas kernels, block(): pl.pallas_call(block_kernel, out_shape=jax.ShapeDtypeStruct((RING, depth,...  172 us

profile of v7, /device:TPU:0, one launch (start us, length us, event | category | flops | bytes accessed | tf_op | source)
XLA Modules:
  0.0 177.6 jit_solution(12909140148773727715)
XLA Ops:
  0.0 1.4 reshape.24.gain_ref
  1.4 1.8 %multiply_sine_fusion = (f32[512,64]{1,0:T(8,128)}, f32[512,64]{1,0:T(8,128)}) fusion(f32[64]{0:T(128)S(1)} %multiply_power_fusion, f32[512]{0:T(512)S(1)} %add_convert_fusion), kind=kLoop, calls=%fused_computation | loop fusion | flops 32768 | bytes 264448 | tf_op jit(solution)/shard_map/sin | solution.py:549
  3.2 171.9 %shard_map.82 = bf16[4,336,512]{2,1,0:T(8,128)(2,1)} custom-call(bf16[1344,512]{1,0:T(8,128)(2,1)} %bitcast.8, f32[1,5376]{1,0:T(1,128)} %reshape.24.gain_ref, bf16[336,1024]{1,0:T(8,128)(2,1)} %wq_ref.1, bf16[336,512]{1,0:T(8,128)(2,1)} %wk_ref.1, bf16[336,512]{1,0:T(8,128)(2,1)} %wv_ref.1, bf16[336,1024]{1,0:T(8,128)(2,1)} %bitcast.9, f32[1,128]{1,0:T(1,128)} %bitcast.10, ...), custom_call_target="tpu_custom_call" | custom-call | tf_op jit(solution)/shard_map/pallas_call | solution.py:512
  175.1 2.5 %copy.10 = bf16[512,1344]{0,1:T(8,128)(2,1)} copy(bf16[512,1344]{0,1:T(8,128)(2,1)} %bitcast.7) | data formatting | bytes 2752512
  (2 shorter events, 0.0 us)
